TPU v7x, 768 devices: a whole 4x8x12 slice. The times are simulated.
768 devices in a mesh: space: 48 (over z, x_lo, core), date: 8 (over y), head: 2 (over x_hi).
Axes of the slice: x: 4 (x_hi: 2, x_lo: 2; x = x_hi * 2 + x_lo), y: 8, z: 12, core: 2. Of those that a mesh axis runs over, the one named last changes fastest.
Arguments:
- latent_queries: bfloat16 [24576, 1536], P('space', 'head'), may hold values from -6 to 6
- grad_attention: bfloat16 [24576, 1536], P('space', 'head'), may hold values from -48 to 48
- cond_tokens: bfloat16 [3072, 1536], P('date'), may hold values from -6 to 6
- w_key: bfloat16 [1536, 1536], P(None, 'head'), may hold values from -0.15625 to 0.15625
- w_value: bfloat16 [1536, 1536], P(None, 'head'), may hold values from -0.15625 to 0.15625
- clear_tokens: int32 [48, 3072], P('space', 'date'), may hold values from 0 to 1, as said below
Outputs:
- grad_queries: bfloat16 [24576, 1536], P(('space', 'date'), 'head')
- grad_cond: bfloat16 [3072, 1536], P('date', ('space', 'head'))
Inputs may be any that keep to these rules, and one draw needn't show every extreme that they name: `clear_tokens`: every tile has at least one clear condition token.
All inputs are finite; a program needn't handle non-finite values.
Results may differ from a plain program's by a relative error of at most 0.024.
Values may be sent and summed in bfloat16 or wider, within the bound.
No kernel may reach another device: no remote copies, remote signals or barrier semaphores. Data moves between devices by JAX's collectives and lax.ppermute only.
A program may use at most 64 MiB of HBM per device.

v0:
```python
import jax
import jax.numpy as jnp
from jax import lax
from jax.sharding import PartitionSpec as P

DH = 64


NORM_EPSILON = 1e-06


def unit_rms(values):
    return values * lax.rsqrt(jnp.mean(values * values, axis=-1, keepdims=True) + NORM_EPSILON)


def unit_rms_back(values, upstream):
    factor = lax.rsqrt(jnp.mean(values * values, axis=-1, keepdims=True) + NORM_EPSILON)
    normed = values * factor
    return factor * (upstream - normed * jnp.mean(upstream * normed, axis=-1, keepdims=True))


def body(latent_queries, grad_attention, cond_tokens, w_key, w_value, clear_tokens):
    lat_rows = latent_queries.shape[0]
    cond_rows = cond_tokens.shape[0]
    local_width = w_key.shape[1]
    local_heads = local_width // DH
    score_scale = DH ** (-0.5)
    q_float = latent_queries.astype(jnp.float32).reshape(lat_rows, local_heads, DH)
    q_heads = unit_rms(q_float).astype(jnp.bfloat16).transpose(1, 0, 2)
    key_raw = (
        jnp.dot(cond_tokens, w_key, preferred_element_type=jnp.float32)
        .reshape(cond_rows, local_heads, DH)
        .transpose(1, 0, 2)
    )
    key_heads = unit_rms(key_raw).astype(jnp.bfloat16)
    value_heads = (
        jnp.dot(cond_tokens, w_value, preferred_element_type=jnp.float32)
        .astype(jnp.bfloat16)
        .reshape(cond_rows, local_heads, DH)
        .transpose(1, 0, 2)
    )
    grad_heads = grad_attention.reshape(lat_rows, local_heads, DH).transpose(1, 0, 2)
    clear_mask = clear_tokens.astype(jnp.float32)

    def weights_of(query_head, key_head, value_head, grad_head):
        scores = (
            jnp.einsum("rd,cd->rc", query_head, key_head, preferred_element_type=jnp.float32)
            * score_scale
        )
        weights = jnp.exp(scores) * clear_mask
        dprob = jnp.einsum("rd,cd->rc", grad_head, value_head, preferred_element_type=jnp.float32)
        return (weights, dprob)

    def first_pass(operands):
        weights, dprob = weights_of(*operands)
        return (jnp.sum(weights, axis=1), jnp.sum(weights * dprob, axis=1))

    part_total, part_carried = lax.map(first_pass, (q_heads, key_heads, value_heads, grad_heads))
    total, carried = (
        lax.psum(part_total.astype(jnp.bfloat16), "date").astype(jnp.float32),
        lax.psum(part_carried.astype(jnp.bfloat16), "date").astype(jnp.float32),
    )

    def second_pass(operands):
        query_head, key_head, value_head, grad_head, total_head, carried_head = operands
        weights, dprob = weights_of(query_head, key_head, value_head, grad_head)
        prob_float = weights / total_head[:, None]
        prob = prob_float.astype(jnp.bfloat16)
        dscore = (prob_float * (dprob - (carried_head / total_head)[:, None])).astype(jnp.bfloat16)
        grad_values = jnp.einsum("rc,rd->cd", prob, grad_head, preferred_element_type=jnp.float32)
        grad_key_unit = (
            jnp.einsum("rc,rd->cd", dscore, query_head, preferred_element_type=jnp.float32)
            * score_scale
        )
        return (dscore, grad_key_unit, grad_values)

    dscore_all, grad_key_unit, grad_values = lax.map(
        second_pass, (q_heads, key_heads, value_heads, grad_heads, total, carried)
    )
    share_rows = lat_rows // lax.axis_size("date")
    term = (
        jnp.einsum("hrc,hcd->rhd", dscore_all, key_heads, preferred_element_type=jnp.float32)
        * score_scale
    )
    grad_q_unit = lax.psum_scatter(
        term.reshape(share_rows * lax.axis_size("date"), local_width).astype(jnp.bfloat16),
        "date",
        scatter_dimension=0,
        tiled=True,
    ).astype(jnp.float32)
    own_queries = lax.dynamic_slice_in_dim(
        q_float, lax.axis_index("date") * share_rows, share_rows, 0
    )
    grad_queries = (
        unit_rms_back(own_queries, grad_q_unit.reshape(share_rows, local_heads, DH))
        .astype(jnp.bfloat16)
        .reshape(share_rows, local_width)
    )
    w_key_heads = w_key.reshape(w_key.shape[0], local_heads, DH)
    w_value_heads = w_value.reshape(w_value.shape[0], local_heads, DH)
    space_count = lax.axis_size("space")
    head_count = lax.axis_size("head")
    key_sum, value_sum = lax.psum((grad_key_unit, grad_values), "space")
    grad_key_raw = unit_rms_back(key_raw, key_sum).astype(jnp.bfloat16)
    grad_value_rows = value_sum.astype(jnp.bfloat16)
    feature_width = w_key.shape[0] // space_count
    feature_offset = lax.axis_index("space") * feature_width
    key_block = lax.dynamic_slice_in_dim(
        w_key_heads, feature_offset, feature_width // head_count * lax.axis_size("head"), 0
    )
    value_block = lax.dynamic_slice_in_dim(
        w_value_heads, feature_offset, feature_width // head_count * lax.axis_size("head"), 0
    )
    summed = lax.psum_scatter(
        (
            jnp.einsum("fhd,hcd->fc", key_block, grad_key_raw, preferred_element_type=jnp.float32)
            + jnp.einsum(
                "fhd,hcd->fc", value_block, grad_value_rows, preferred_element_type=jnp.float32
            )
        ).astype(jnp.bfloat16),
        "head",
        scatter_dimension=0,
        tiled=True,
    ).astype(jnp.float32)
    grad_cond = summed.T.astype(jnp.bfloat16)
    return (grad_queries, grad_cond)


def solution(mesh):
    return jax.shard_map(
        body,
        mesh=mesh,
        in_specs=(
            P("space", "head"),
            P("space", "head"),
            P("date", None),
            P(None, "head"),
            P(None, "head"),
            P("space", "date"),
        ),
        out_specs=(P(("space", "date"), "head"), P("date", ("space", "head"))),
        check_vma=False,
    )
```

profile of v0, /device:TPU:6, one launch (start us, length us, event | category | flops | bytes accessed | tf_op | source)
XLA Modules:
  0.0 555.6 jit_solution(14810434769884181589)
XLA Ops:
  9.3 3.1 fusion.49
  13.5 1.4 copy.22
  14.9 1.4 copy.13
  17.7 2.5 copy.21
  20.2 2.3 copy.15
  22.5 2.4 copy.19
  24.9 3.6 convolution_convert_fusion
  28.5 2.2 copy.16
  30.7 2.3 copy.20
  33.0 31.8 %while.26 = (s32[]{:T(128)}, bf16[12,512]{1,0:T(8,128)(2,1)S(1)}, bf16[12,512]{1,0:T(8,128)(2,1)S(1)}, bf16[12,512,64]{2,1,0:T(8,128)(2,1)}, bf16[12,384,64]{2,1...) while((s32[]{:T(128)}, bf16[12,512]{1,0:T(8,128)(2,1)S(1)}, ...), condition=%wide.region_6.7_spmd, body=%wide.region_3.6_spmd.sunk | while | flops 51313664 | bytes 2050681 | solution.py:58
  35.7 1.3 fusion.73
  41.0 1.3 fusion.73
  43.6 1.3 fusion.73
  51.6 1.3 fusion.73
  62.2 1.3 fusion.73
  64.8 30.4 %all-reduce = (bf16[12,512]{1,0:T(8,128)(2,1)S(1)}, bf16[12,512]{1,0:T(8,128)(2,1)S(1)}) all-reduce(bf16[12,512]{1,0:T(8,128)(2,1)S(1)} %get-tuple-element.104, bf16[12,512]{1,0:T(8,128)(2,1)S(1)} %get-tuple-element.105), channel_id=1, replica_groups=mesh['space'=48,'date'=8,'head'=2] {'date'}, use_global_device_ids=true, to_apply=%region_7.8 | all-reduce | flops 12288 | bytes 49152 | tf_op jit(solution)/shard_map/psum | solution.py:60
  95.2 82.5 %while.27 = (s32[]{:T(128)}, bf16[12,512,384]{2,1,0:T(8,128)(2,1)}, f32[12,384,64]{1,2,0:T(8,128)}, f32[12,384,64]{1,2,0:T(8,128)}, bf16[12,512,64]{2,1,0:T(8,12...) while((s32[]{:T(128)}, bf16[12,512,384]{2,1,0:T(8,128)(2,1)}, ...), condition=%wide.region_10.11_spmd, body=%wide.region_9.10_spmd.sunk | while | flops 102064640 | bytes 4484229 | solution.py:77
  96.6 2.0 bitcast_dynamic-update-slice_fusion.2
  98.5 1.8 fusion.82
  100.3 1.8 fusion.83
  103.4 2.0 bitcast_dynamic-update-slice_fusion.2
  105.4 1.8 fusion.82
  107.2 1.8 fusion.83
  110.3 2.0 bitcast_dynamic-update-slice_fusion.2
  112.3 1.8 fusion.82
  114.1 1.8 fusion.83
  117.2 2.0 bitcast_dynamic-update-slice_fusion.2
  119.2 1.8 fusion.82
  121.0 1.8 fusion.83
  124.1 2.0 bitcast_dynamic-update-slice_fusion.2
  126.0 1.8 fusion.82
  127.8 1.8 fusion.83
  130.9 2.0 bitcast_dynamic-update-slice_fusion.2
  132.9 1.8 fusion.82
  134.7 1.8 fusion.83
  137.8 2.0 bitcast_dynamic-update-slice_fusion.2
  139.8 1.8 fusion.82
  141.6 1.8 fusion.83
  144.7 2.0 bitcast_dynamic-update-slice_fusion.2
  146.7 1.8 fusion.82
  148.4 1.8 fusion.83
  151.5 2.0 bitcast_dynamic-update-slice_fusion.2
  153.5 1.8 fusion.82
  155.3 1.8 fusion.83
  158.4 2.0 bitcast_dynamic-update-slice_fusion.2
  160.4 1.8 fusion.82
  162.2 1.8 fusion.83
  165.3 2.0 bitcast_dynamic-update-slice_fusion.2
  167.3 1.8 fusion.82
  169.1 1.8 fusion.83
  172.2 2.0 bitcast_dynamic-update-slice_fusion.2
  174.1 1.8 fusion.82
  175.9 1.8 fusion.83
  177.8 5.0 multiply_convert_fusion
  182.8 2.3 copy.25
  185.2 174.7 %all-reduce.5 = bf16[12,384,64]{1,2,0:T(8,128)(2,1)} all-reduce(f32[12,384,64]{1,2,0:T(8,128)} %get-tuple-element.108), channel_id=1, replica_groups=mesh['space'=48,'date'=8,'head'=2] {'space'}, use_global_device_ids=true, to_apply=%region_15.16 | all-reduce | flops 294912 | bytes 1769472 | tf_op jit(solution)/shard_map/psum | solution.py:103
  359.9 4.3 copy.29
  364.2 4.3 copy.31
  368.5 1.4 convert.2
  371.1 148.6 %all-reduce.4.cloned.1.call-done = f32[12,384,64]{1,2,0:T(8,128)} async-done(((f32[12,384,64]{1,2,0:T(8,128)}), f32[12,384,64]{1,2,0:T(8,128)}) %all-reduce.4.cloned.1.call-update) | async-done | bytes 1179664 | tf_op jit(solution)/shard_map/psum | solution.py:103
  519.7 1.6 multiply_reduce_fusion.1
  521.3 1.4 convolution_bitcast_fusion.2
  522.7 1.9 fusion.39
  528.8 19.4 %reduce-scatter.5.cloned.1.call-done = bf16[16,384]{1,0:T(8,128)(2,1)} async-done(((bf16[32,384]{1,0:T(8,128)(2,1)}), bf16[16,384]{1,0:T(8,128)(2,1)}) %reduce-scatter.5.cloned.1.call-update) | async-done | bytes 12304 | tf_op jit(solution)/shard_map/reduce_scatter | solution.py:114
  (142 shorter events, 49.8 us)
Async XLA Ops:
  8.0 1.3 copy-start
  8.0 511.7 %all-reduce.4.cloned.1.call-start = ((), (), s32[]{:S(2)}) async-start(), calls=%async_computation.3 | async-start | bytes 2359296 | tf_op jit(solution)/shard_map/psum | solution.py:103
  12.6 0.8 copy-start.1
  30.7 2.3 copy-start.4
  177.7 346.9 %reduce-scatter.3.cloned.1.call-start = ((), (), s32[]{:S(2)}) async-start(), calls=%async_computation.2 | async-start | bytes 884736 | tf_op jit(solution)/shard_map/reduce_scatter | solution.py:85
  185.1 363.0 %reduce-scatter.5.cloned.1.call-start = ((), (), s32[]{:S(2)}) async-start(), calls=%async_computation.4 | async-start | bytes 36864 | tf_op jit(solution)/shard_map/reduce_scatter | solution.py:114
  519.7 1.6 copy-start.2
  521.3 1.4 copy-start.3
Sparse Core Ops, SparseCore 0:
  177.9 341.7 all-reduce.3
Sparse Core Ops, SparseCore 1:
  185.2 46.8 reduce-scatter.2
  524.7 23.5 reduce-scatter.4
where the time goes:
time: 560 us; the launch traced here: 556 us
  blocking collectives  205 us (37%)
  waiting for transfers between devices  168 us (30%)
  matrix products  127 us (23%)
  local copies, waits for them, and re-layouts  30.4 us (5%)
  between operations  15.7 us (3%)
  other arithmetic  8.62 us (2%)
    psum x1, blocking collectives, body(): key_sum, value_sum = lax.psum((grad_key_unit, grad_values), 'space')  175 us
    psum x1, waiting for transfers between devices, body(): key_sum, value_sum = lax.psum((grad_key_unit, grad_values), 'space')  149 us
    dot_general x24, matrix products, weights_of(): jnp.einsum('rd,cd->rc', grad_head, value_head, preferred_element_type=jnp...  38.6 us
    dot_general x24, matrix products, weights_of(): jnp.einsum('rd,cd->rc', query_head, key_head, preferred_element_type=jnp....  30.5 us
    psum x1, blocking collectives, body(): lax.psum(part_total.astype(jnp.bfloat16), 'date').astype(jnp.float32)  30.4 us
    dot_general x12, matrix products, second_pass(): jnp.einsum('rc,rd->cd', dscore, query_head, preferred_element_type=jnp.fl...  21.4 us
    dot_general x12, matrix products, second_pass(): jnp.einsum('rc,rd->cd', prob, grad_head, preferred_element_type=jnp.float32)  21.4 us
    reduce_scatter x1, waiting for transfers between devices, body(): lax.psum_scatter((jnp.einsum('fhd,hcd->fc', key_block, grad_key_raw, pref...  19.4 us
  transfers between devices with their start and end apart: 3, of which 2 were waited for; matrix products, arithmetic and copies ran while one was open for 5% of the time, Pallas kernels for 0%

commit v1 on v0

v1 whole, which is shorter than its diff:
```python
import jax
import jax.numpy as jnp
from jax import lax
from jax.experimental import pallas as pl
from jax.experimental.pallas import tpu as pltpu
from jax.sharding import Mesh, PartitionSpec as P

DH = 64
PAIR = 2 * DH
SPACE = ("z", "x", "core")
NEAR = ("x", "core", "head")

NORM_EPSILON = 1e-06

NT = (((1,), (1,)), ((), ()))
NN = (((1,), (0,)), ((), ()))


def dot(a, b, dims=NN):
    return lax.dot_general(a, b, dims, preferred_element_type=jnp.float32)


def head_mean(x, ones):
    high = x.astype(jnp.bfloat16)
    low = (x - high.astype(jnp.float32)).astype(jnp.bfloat16)
    return dot(jnp.concatenate([high, low], axis=1), ones) * (1.0 / DH)


def ones_of_heads():
    row = lax.broadcasted_iota(jnp.int32, (2 * PAIR, PAIR), 0) % PAIR
    column = lax.broadcasted_iota(jnp.int32, (2 * PAIR, PAIR), 1)
    return ((row < DH) == (column < DH)).astype(jnp.bfloat16)


def split_heads(x):
    lane = lax.broadcasted_iota(jnp.int32, x.shape, 1)
    zero = jnp.zeros_like(x)
    return jnp.concatenate([jnp.where(lane < DH, x, zero), jnp.where(lane < DH, zero, x)], axis=0)


def scores_kernel(q_ref, g_ref, cond_ref, wk_ref, wv_ref, mask_ref, w_ref, e_ref, sums_ref, keys_ref):
    cond_rows = cond_ref.shape[0]
    ones = ones_of_heads()
    projected = dot(cond_ref[...], jnp.concatenate([wk_ref[...], wv_ref[...]], axis=1))
    key_raw = projected[:, :PAIR]
    keys_ref[...] = key_raw
    key_unit = (key_raw * lax.rsqrt(head_mean(key_raw * key_raw, ones) + NORM_EPSILON)).astype(jnp.bfloat16)
    values = projected[:, PAIR:].astype(jnp.bfloat16)
    q = q_ref[...].astype(jnp.float32)
    q_unit = (q * lax.rsqrt(head_mean(q * q, ones) + NORM_EPSILON)).astype(jnp.bfloat16)
    scores = dot(split_heads(key_unit), q_unit, NT) * (DH ** -0.5)
    dprob = dot(split_heads(values), g_ref[...], NT)
    mask = mask_ref[...]
    sums = []
    for head in range(2):
        own = slice(head * cond_rows, (head + 1) * cond_rows)
        weights = jnp.exp(scores[own]) * mask
        carried = weights * dprob[own]
        w_ref[head] = weights.astype(jnp.bfloat16)
        e_ref[head] = carried.astype(jnp.bfloat16)
        sums += [jnp.sum(weights, axis=0, keepdims=True), jnp.sum(carried, axis=0, keepdims=True)]
    sums_ref[...] = jnp.broadcast_to(
        jnp.concatenate(sums, axis=0).astype(sums_ref.dtype)[None, None], sums_ref.shape
    )


def grads_kernel(q_ref, g_ref, keys_ref, wk_ref, wv_ref, w_ref, e_ref, sums_ref, gq_ref, gc_ref, acc_ref):
    cond_rows = keys_ref.shape[0]
    ones = ones_of_heads()
    q = q_ref[...].astype(jnp.float32)
    q_factor = lax.rsqrt(head_mean(q * q, ones) + NORM_EPSILON)
    q_normed = q * q_factor
    q_unit = q_normed.astype(jnp.bfloat16)
    key_raw = keys_ref[...]
    key_factor = lax.rsqrt(head_mean(key_raw * key_raw, ones) + NORM_EPSILON)
    key_normed = key_raw * key_factor
    keys_turned = key_normed.T.astype(jnp.bfloat16)
    g = g_ref[...]
    grad_values = []
    grad_keys = []
    grad_q = []
    sums = jnp.sum(sums_ref[:, 0].astype(jnp.float32), axis=0)
    for head in range(2):
        total = sums[2 * head : 2 * head + 1, :]
        carried = sums[2 * head + 1 : 2 * head + 2, :]
        inverse = 1.0 / total
        mean = carried * inverse
        weights = w_ref[head].astype(jnp.float32)
        prob = (weights * inverse).astype(jnp.bfloat16)
        dscore = ((e_ref[head].astype(jnp.float32) - weights * mean) * inverse).astype(jnp.bfloat16)
        grad_values.append(dot(prob, g))
        grad_keys.append(dot(dscore, q_unit))
        grad_q.append(dot(keys_turned[head * DH : (head + 1) * DH], dscore))
    lane = lax.broadcasted_iota(jnp.int32, (cond_rows, PAIR), 1)
    gv = jnp.where(lane < DH, grad_values[0], grad_values[1])
    gk = jnp.where(lane < DH, grad_keys[0], grad_keys[1]) * (DH ** -0.5)
    gq = jnp.concatenate(grad_q, axis=0).T * (DH ** -0.5)
    gq_back = q_factor * (gq - q_normed * head_mean(gq * q_normed, ones))
    gq_ref[...] = gq_back.astype(gq_ref.dtype)
    gk_back = key_factor * (gk - key_normed * head_mean(gk * key_normed, ones))
    both = jnp.concatenate([gk_back.astype(jnp.bfloat16), gv.astype(jnp.bfloat16)], axis=1)
    part = dot(jnp.concatenate([wk_ref[...], wv_ref[...]], axis=1), both, NT)
    step = pl.program_id(0)

    @pl.when(step == 0)
    def _():
        acc_ref[...] = part

    @pl.when(step > 0)
    def _():
        acc_ref[...] += part

    @pl.when(step == pl.num_programs(0) - 1)
    def _():
        near, far, own = gc_ref.shape[:3]
        for i in range(far):
            for j in range(near):
                start = (i * near + j) * own
                gc_ref[j, i] = acc_ref[start : start + own, :].astype(gc_ref.dtype)


def columns(rows):
    return pl.BlockSpec((rows, PAIR), lambda i: (0, i))


def whole(shape):
    return pl.BlockSpec(shape, lambda i: (0,) * len(shape), pipeline_mode=pl.Buffered(1))


def body(latent_queries, grad_attention, cond_tokens, w_key, w_value, clear_tokens):
    lat_rows, local_width = latent_queries.shape
    cond_rows, width = cond_tokens.shape
    pairs = local_width // PAIR
    mask = clear_tokens.astype(jnp.float32).reshape(cond_rows, 1)
    params = pltpu.CompilerParams(
        dimension_semantics=("arbitrary",), vmem_limit_bytes=56 * 1024 * 1024
    )
    score_block = pl.BlockSpec((2, cond_rows, lat_rows), lambda i: (i, 0, 0))
    dates = lax.axis_size("date")
    far = lax.axis_size("z")
    near = lax.axis_size(NEAR)
    own = width // (far * near)
    sums_block = pl.BlockSpec((dates, 1, 4, lat_rows), lambda i: (0, i, 0, 0))
    weights, carried, sums, key_raw = pl.pallas_call(
        scores_kernel,
        grid=(pairs,),
        in_specs=[
            columns(lat_rows),
            columns(lat_rows),
            whole((cond_rows, width)),
            columns(width),
            columns(width),
            whole((cond_rows, 1)),
        ],
        out_specs=[score_block, score_block, sums_block, columns(cond_rows)],
        out_shape=[
            jax.ShapeDtypeStruct((2 * pairs, cond_rows, lat_rows), jnp.bfloat16),
            jax.ShapeDtypeStruct((2 * pairs, cond_rows, lat_rows), jnp.bfloat16),
            jax.ShapeDtypeStruct((dates, pairs, 4, lat_rows), jnp.bfloat16),
            jax.ShapeDtypeStruct((cond_rows, local_width), jnp.float32),
        ],
        compiler_params=params,
        name="scores",
    )(latent_queries, grad_attention, cond_tokens, w_key, w_value, mask)
    sums = lax.all_to_all(sums, "date", 0, 0, tiled=True)
    grad_q, grad_c = pl.pallas_call(
        grads_kernel,
        grid=(pairs,),
        in_specs=[
            columns(lat_rows),
            columns(lat_rows),
            columns(cond_rows),
            columns(width),
            columns(width),
            score_block,
            score_block,
            sums_block,
        ],
        out_specs=[columns(lat_rows), whole((near, far, own, cond_rows))],
        out_shape=[
            jax.ShapeDtypeStruct((lat_rows, local_width), jnp.bfloat16),
            jax.ShapeDtypeStruct((near, far, own, cond_rows), jnp.bfloat16),
        ],
        scratch_shapes=[pltpu.VMEM((width, cond_rows), jnp.float32)],
        compiler_params=params,
        name="grads",
    )(latent_queries, grad_attention, key_raw, w_key, w_value, weights, carried, sums)
    grad_queries = lax.psum_scatter(grad_q, "date", scatter_dimension=0, tiled=True)
    near_parts = lax.all_to_all(grad_c, NEAR, 0, 0, tiled=True)
    near_sum = jnp.sum(near_parts.astype(jnp.float32), axis=0).astype(jnp.bfloat16)
    far_parts = lax.all_to_all(near_sum, "z", 0, 0, tiled=True)
    grad_cond = jnp.sum(far_parts.astype(jnp.float32), axis=0)
    return (grad_queries, grad_cond.T.astype(jnp.bfloat16))


def solution(mesh):
    space, dates, heads = mesh.devices.shape
    split = Mesh(
        mesh.devices.reshape(space // 4, 2, 2, dates, heads), ("z", "x", "core", "date", "head")
    )
    return jax.shard_map(
        body,
        mesh=split,
        in_specs=(
            P(SPACE, "head"),
            P(SPACE, "head"),
            P("date", None),
            P(None, "head"),
            P(None, "head"),
            P(SPACE, "date"),
        ),
        out_specs=(P(SPACE + ("date",), "head"), P("date", SPACE + ("head",))),
        check_vma=False,
    )
```

time: 560 us -> 110 us (0.20)
  waiting for transfers between devices: 168 us -> 0.02 us
  blocking collectives: 205 us -> 64.7 us
  matrix products: 127 us -> 0 us
  local copies, waits for them, and re-layouts: 30.4 us -> 0.83 us
  Pallas kernels: 0 us -> 27.5 us
  other arithmetic: 8.62 us -> 1.48 us
    psum x2 -> x0, blocking collectives: 205 us -> none  [the longest x1 175 us: body(): key_sum, value_sum = lax.psum((grad_key_unit, grad_values), 'space')]
    psum x1 -> x0, waiting for transfers between devices: 149 us -> none  [body(): key_sum, value_sum = lax.psum((grad_key_unit, grad_values), 'space')]
    dot_general x77 -> x0, matrix products: 127 us -> none  [the longest x24 38.6 us: weights_of(): jnp.einsum('rd,cd->rc', grad_head, value_head, preferred_element_type=jnp...]
    all_to_all x0 -> x3, blocking collectives: none -> 64.7 us  [the longest x1 24.2 us: body(): near_parts = lax.all_to_all(grad_c, NEAR, 0, 0, tiled=True)]
    pallas_call x0 -> x2, Pallas kernels: none -> 27.5 us  [the longest x1 14.1 us: body(): pl.pallas_call(grads_kernel, grid=(pairs,), in_specs=[columns(lat_rows),...]
    reduce_scatter x2 -> x1, waiting for transfers between devices: 19.4 us -> 0.01 us  [body(): lax.psum_scatter(grad_q, 'date', scatter_dimension=0, tiled=True)]
    unnamed x14 -> x0, local copies, waits for them, and re-layouts: 14.3 us -> none
    while x4 -> x0, local copies, waits for them, and re-layouts: 8.68 us -> none  [the longest x2 4.73 us: body(): lax.map(first_pass, (q_heads, key_heads, value_heads, grad_heads))]
  transfers between devices with their start and end apart: 3 -> 1, of which waited for: 2 -> 0; matrix products, arithmetic and copies ran while one was open for 5% -> 1% of each run, Pallas kernels for 0% -> 0%
where the time goes in v1:
time: 110 us; the launch traced here: 109 us
  blocking collectives  64.7 us (59%)
  Pallas kernels  27.5 us (25%)
  between operations  14 us (13%)
  other arithmetic  1.48 us (1%)
    all_to_all x1, blocking collectives, body(): near_parts = lax.all_to_all(grad_c, NEAR, 0, 0, tiled=True)  24.2 us
    all_to_all x1, blocking collectives, body(): far_parts = lax.all_to_all(near_sum, 'z', 0, 0, tiled=True)  22.8 us
    all_to_all x1, blocking collectives, body(): sums = lax.all_to_all(sums, 'date', 0, 0, tiled=True)  17.7 us
    pallas_call x1, Pallas kernels, body(): pl.pallas_call(grads_kernel, grid=(pairs,), in_specs=[columns(lat_rows),...  14.1 us
    pallas_call x1, Pallas kernels, body(): pl.pallas_call(scores_kernel, grid=(pairs,), in_specs=[columns(lat_rows),...  13.4 us
  transfers between devices with their start and end apart: 1, of which 0 were waited for; matrix products, arithmetic and copies ran while one was open for 1% of the time, Pallas kernels for 0%

profile of v1, /device:TPU:6, one launch (start us, length us, event | category | flops | bytes accessed | tf_op | source)
XLA Modules:
  0.0 108.6 jit_solution(16727674397554405720)
XLA Ops:
  7.2 0.0 reduce-scatter.2.cloned.1.call-start
  7.2 0.7 convert_bitcast_fusion
  7.9 0.8 copy.9.mask_ref
  8.7 13.4 %scores.1 = (bf16[12,384,512]{2,1,0:T(8,128)(2,1)}, bf16[12,384,512]{2,1,0:T(8,128)(2,1)}, bf16[8,6,4,512]{3,2,1,0:T(4,128)(2,1)}, f32[384,768]{1,0:T(8,128)}) custom-call(bf16[512,768]{1,0:T(8,128)(2,1)} %q_ref.3, bf16[512,768]{1,0:T(8,128)(2,1)} %g_ref.3, bf16[384,1536]{1,0:T(8,128)(2,1)} %cond_ref.1, bf16[1536,768]{1,0:T(8,128)(2,1)} %wk_ref.3, ...), custom_call_target="tpu_custom_call" | custom-call | tf_op jit(solution)/shard_map/scores/pallas_call | solution.py:144
  22.1 17.7 %all_to_all.15.sums_ref = bf16[8,6,4,512]{3,2,1,0:T(4,128)(2,1)} all-to-all(bf16[8,6,4,512]{3,2,1,0:T(4,128)(2,1)} %get-tuple-element.11), channel_id=1, replica_groups=mesh['z'=12,'x'=2,'core'=2,'date'=8,'head'=2] {'date'}, dimensions={0} | all-to-all | bytes 393216 | tf_op jit(solution)/shard_map/all_to_all | solution.py:165
  39.8 14.1 %grads.1 = (bf16[512,768]{1,0:T(8,128)(2,1)}, bf16[8,12,16,384]{3,2,1,0:T(8,128)(2,1)}) custom-call(bf16[512,768]{1,0:T(8,128)(2,1)} %q_ref.3, bf16[512,768]{1,0:T(8,128)(2,1)} %g_ref.3, f32[384,768]{1,0:T(8,128)} %get-tuple-element.8.keys_ref, bf16[1536,768]{1,0:T(8,128)(2,1)} %wk_ref.3, bf16[1536,768]{1,0:T(8,128)(2,1)} %wv_ref.3, ...), custom_call_target="tpu_custom_call" | custom-call | tf_op jit(solution)/shard_map/grads/pallas_call | solution.py:166
  53.9 0.0 reduce-scatter.2.cloned.1.call-update
  53.9 24.2 %all_to_all.16 = bf16[8,12,16,384]{3,2,1,0:T(8,128)(2,1)S(1)} all-to-all(bf16[8,12,16,384]{3,2,1,0:T(8,128)(2,1)} %get-tuple-element.13), channel_id=1, replica_groups=mesh['z'=12,'x'=2,'core'=2,'date'=8,'head'=2] {'x','core','head'}, dimensions={0} | all-to-all | bytes 2359296 | tf_op jit(solution)/shard_map/all_to_all | solution.py:189
  78.1 0.2 reduce_sum.24
  78.2 22.8 %all_to_all.17 = bf16[12,16,384]{2,1,0:T(8,128)(2,1)S(1)} all-to-all(bf16[12,16,384]{2,1,0:T(8,128)(2,1)S(1)} %reduce_sum.24), channel_id=1, replica_groups=mesh['z'=12,'x'=2,'core'=2,'date'=8,'head'=2] {'z'}, dimensions={0} | all-to-all | bytes 294912 | tf_op jit(solution)/shard_map/all_to_all | solution.py:191
  101.1 0.6 reduce_sum.25
  101.7 0.0 reduce-scatter.2.cloned.1.call-done
Async XLA Ops:
  7.2 94.6 %reduce-scatter.2.cloned.1.call-start = ((), (), s32[]{:S(2)}) async-start(), calls=%async_computation.4 | async-start | bytes 884736 | tf_op jit(solution)/shard_map/reduce_scatter | solution.py:188
Sparse Core Ops, SparseCore 0:
  54.0 44.2 reduce-scatter.1

commit v2 on v1

--- a/solution.py
+++ b/solution.py
@@ -8,7 +8,7 @@
 DH = 64
 PAIR = 2 * DH
 SPACE = ("z", "x", "core")
-NEAR = ("x", "core", "head")
+CHIPS = ("x", "head")
 
 NORM_EPSILON = 1e-06
 
@@ -38,8 +38,14 @@
     return jnp.concatenate([jnp.where(lane < DH, x, zero), jnp.where(lane < DH, zero, x)], axis=0)
 
 
-def scores_kernel(q_ref, g_ref, cond_ref, wk_ref, wv_ref, mask_ref, w_ref, e_ref, sums_ref, keys_ref):
+def scores_kernel(q_ref, g_ref, cond_ref, wk_ref, wv_ref, clear_ref, w_ref, e_ref, sums_ref, keys_ref, mask_ref):
     cond_rows = cond_ref.shape[0]
+    lat_rows = q_ref.shape[0]
+
+    @pl.when(pl.program_id(0) == 0)
+    def _():
+        mask_ref[...] = jnp.broadcast_to(clear_ref[...].astype(jnp.float32), (PAIR, cond_rows)).T
+
     ones = ones_of_heads()
     projected = dot(cond_ref[...], jnp.concatenate([wk_ref[...], wv_ref[...]], axis=1))
     key_raw = projected[:, :PAIR]
@@ -50,7 +56,7 @@
     q_unit = (q * lax.rsqrt(head_mean(q * q, ones) + NORM_EPSILON)).astype(jnp.bfloat16)
     scores = dot(split_heads(key_unit), q_unit, NT) * (DH ** -0.5)
     dprob = dot(split_heads(values), g_ref[...], NT)
-    mask = mask_ref[...]
+    mask = jnp.concatenate([mask_ref[...]] * (lat_rows // PAIR), axis=1)
     sums = []
     for head in range(2):
         own = slice(head * cond_rows, (head + 1) * cond_rows)
@@ -64,7 +70,21 @@
     )
 
 
-def grads_kernel(q_ref, g_ref, keys_ref, wk_ref, wv_ref, w_ref, e_ref, sums_ref, gq_ref, gc_ref, acc_ref):
+def queries_kernel(keys_ref, w_ref, e_ref, plain_ref, carried_ref):
+    ones = ones_of_heads()
+    key_raw = keys_ref[...]
+    key_unit = key_raw * lax.rsqrt(head_mean(key_raw * key_raw, ones) + NORM_EPSILON)
+    turned = key_unit.T.astype(jnp.bfloat16)
+    for head in range(2):
+        own = turned[head * DH : (head + 1) * DH]
+        plain_ref[head] = dot(own, w_ref[head])
+        carried_ref[head] = dot(own, e_ref[head])
+
+
+def grads_kernel(
+    place_ref, q_ref, g_ref, keys_ref, wk_ref, wv_ref, w_ref, e_ref, plain_ref, carried_ref, sums_ref,
+    gq_ref, keep_ref, send_ref, acc_ref
+):
     cond_rows = keys_ref.shape[0]
     ones = ones_of_heads()
     q = q_ref[...].astype(jnp.float32)
@@ -74,12 +94,11 @@
     key_raw = keys_ref[...]
     key_factor = lax.rsqrt(head_mean(key_raw * key_raw, ones) + NORM_EPSILON)
     key_normed = key_raw * key_factor
-    keys_turned = key_normed.T.astype(jnp.bfloat16)
     g = g_ref[...]
     grad_values = []
     grad_keys = []
     grad_q = []
-    sums = jnp.sum(sums_ref[:, 0].astype(jnp.float32), axis=0)
+    sums = jnp.sum(sums_ref[:, pl.program_id(0)].astype(jnp.float32), axis=0)
     for head in range(2):
         total = sums[2 * head : 2 * head + 1, :]
         carried = sums[2 * head + 1 : 2 * head + 2, :]
@@ -90,7 +109,7 @@
         dscore = ((e_ref[head].astype(jnp.float32) - weights * mean) * inverse).astype(jnp.bfloat16)
         grad_values.append(dot(prob, g))
         grad_keys.append(dot(dscore, q_unit))
-        grad_q.append(dot(keys_turned[head * DH : (head + 1) * DH], dscore))
+        grad_q.append((carried_ref[head] - plain_ref[head] * mean) * inverse)
     lane = lax.broadcasted_iota(jnp.int32, (cond_rows, PAIR), 1)
     gv = jnp.where(lane < DH, grad_values[0], grad_values[1])
     gk = jnp.where(lane < DH, grad_keys[0], grad_keys[1]) * (DH ** -0.5)
@@ -112,11 +131,16 @@
 
     @pl.when(step == pl.num_programs(0) - 1)
     def _():
-        near, far, own = gc_ref.shape[:3]
-        for i in range(far):
-            for j in range(near):
-                start = (i * near + j) * own
-                gc_ref[j, i] = acc_ref[start : start + own, :].astype(gc_ref.dtype)
+        chips, far, own = keep_ref.shape[:3]
+        x, core, head = place_ref[0], place_ref[1], place_ref[2]
+        for chip in range(chips):
+            to_x = x ^ (chip // 2)
+            to_head = head ^ (chip % 2)
+            for ref, to_core in ((keep_ref, core), (send_ref, core ^ 1)):
+                near = (to_x * 2 + to_core) * 2 + to_head
+                for i in range(far):
+                    start = pl.multiple_of((i * 8 + near) * own, own)
+                    ref[chip, i] = acc_ref[pl.ds(start, own), :].astype(ref.dtype)
 
 
 def columns(rows):
@@ -125,22 +149,29 @@
 
 def whole(shape):
     return pl.BlockSpec(shape, lambda i: (0,) * len(shape), pipeline_mode=pl.Buffered(1))
+
+
+def add(*parts):
+    return sum(part.astype(jnp.float32) for part in parts).astype(jnp.bfloat16)
 
 
 def body(latent_queries, grad_attention, cond_tokens, w_key, w_value, clear_tokens):
     lat_rows, local_width = latent_queries.shape
     cond_rows, width = cond_tokens.shape
     pairs = local_width // PAIR
-    mask = clear_tokens.astype(jnp.float32).reshape(cond_rows, 1)
+    dates = lax.axis_size("date")
+    far = lax.axis_size("z")
+    chips = lax.axis_size(CHIPS)
+    own = width // (far * chips * 2)
     params = pltpu.CompilerParams(
         dimension_semantics=("arbitrary",), vmem_limit_bytes=56 * 1024 * 1024
     )
     score_block = pl.BlockSpec((2, cond_rows, lat_rows), lambda i: (i, 0, 0))
-    dates = lax.axis_size("date")
-    far = lax.axis_size("z")
-    near = lax.axis_size(NEAR)
-    own = width // (far * near)
+    query_block = pl.BlockSpec((2, DH, lat_rows), lambda i: (i, 0, 0))
     sums_block = pl.BlockSpec((dates, 1, 4, lat_rows), lambda i: (0, i, 0, 0))
+    score_shape = jax.ShapeDtypeStruct((2 * pairs, cond_rows, lat_rows), jnp.bfloat16)
+    query_shape = jax.ShapeDtypeStruct((2 * pairs, DH, lat_rows), jnp.float32)
+    piece_shape = jax.ShapeDtypeStruct((chips, far, own, cond_rows), jnp.bfloat16)
     weights, carried, sums, key_raw = pl.pallas_call(
         scores_kernel,
         grid=(pairs,),
@@ -150,23 +181,35 @@
             whole((cond_rows, width)),
             columns(width),
             columns(width),
-            whole((cond_rows, 1)),
+            whole((1, cond_rows)),
         ],
         out_specs=[score_block, score_block, sums_block, columns(cond_rows)],
         out_shape=[
-            jax.ShapeDtypeStruct((2 * pairs, cond_rows, lat_rows), jnp.bfloat16),
-            jax.ShapeDtypeStruct((2 * pairs, cond_rows, lat_rows), jnp.bfloat16),
+            score_shape,
+            score_shape,
             jax.ShapeDtypeStruct((dates, pairs, 4, lat_rows), jnp.bfloat16),
             jax.ShapeDtypeStruct((cond_rows, local_width), jnp.float32),
         ],
+        scratch_shapes=[pltpu.VMEM((cond_rows, PAIR), jnp.float32)],
         compiler_params=params,
         name="scores",
-    )(latent_queries, grad_attention, cond_tokens, w_key, w_value, mask)
+    )(latent_queries, grad_attention, cond_tokens, w_key, w_value, clear_tokens)
     sums = lax.all_to_all(sums, "date", 0, 0, tiled=True)
-    grad_q, grad_c = pl.pallas_call(
+    plain_q, carried_q = pl.pallas_call(
+        queries_kernel,
+        grid=(pairs,),
+        in_specs=[columns(cond_rows), score_block, score_block],
+        out_specs=[query_block, query_block],
+        out_shape=[query_shape, query_shape],
+        compiler_params=params,
+        name="queries",
+    )(key_raw, weights, carried)
+    place = jnp.stack([lax.axis_index("x"), lax.axis_index("core"), lax.axis_index("head")])
+    grad_q, keep, send = pl.pallas_call(
         grads_kernel,
         grid=(pairs,),
         in_specs=[
+            pl.BlockSpec(memory_space=pltpu.SMEM),
             columns(lat_rows),
             columns(lat_rows),
             columns(cond_rows),
@@ -174,21 +217,35 @@
             columns(width),
             score_block,
             score_block,
-            sums_block,
-        ],
-        out_specs=[columns(lat_rows), whole((near, far, own, cond_rows))],
+            query_block,
+            query_block,
+            pl.BlockSpec(memory_space=pltpu.VMEM),
+        ],
+        out_specs=[columns(lat_rows), whole(piece_shape.shape), whole(piece_shape.shape)],
         out_shape=[
             jax.ShapeDtypeStruct((lat_rows, local_width), jnp.bfloat16),
-            jax.ShapeDtypeStruct((near, far, own, cond_rows), jnp.bfloat16),
+            piece_shape,
+            piece_shape,
         ],
         scratch_shapes=[pltpu.VMEM((width, cond_rows), jnp.float32)],
         compiler_params=params,
         name="grads",
-    )(latent_queries, grad_attention, key_raw, w_key, w_value, weights, carried, sums)
-    grad_queries = lax.psum_scatter(grad_q, "date", scatter_dimension=0, tiled=True)
-    near_parts = lax.all_to_all(grad_c, NEAR, 0, 0, tiled=True)
-    near_sum = jnp.sum(near_parts.astype(jnp.float32), axis=0).astype(jnp.bfloat16)
+    )(
+        place, latent_queries, grad_attention, key_raw, w_key, w_value,
+        weights, carried, plain_q, carried_q, sums,
+    )
+    share_parts = lax.all_to_all(
+        grad_q.reshape(dates, lat_rows // dates, local_width), "date", 0, 0, tiled=True
+    )
+    other = lax.ppermute(send, "core", [(0, 1), (1, 0)])
+    halves = [add(keep[chip], other[chip]) for chip in range(chips)]
+    near_parts = halves[:1] + [
+        lax.ppermute(halves[chip], CHIPS, [(i, i ^ chip) for i in range(chips)])
+        for chip in range(1, chips)
+    ]
+    near_sum, share_parts = lax.optimization_barrier((add(*near_parts), share_parts))
     far_parts = lax.all_to_all(near_sum, "z", 0, 0, tiled=True)
+    grad_queries = jnp.sum(share_parts.astype(jnp.float32), axis=0).astype(jnp.bfloat16)
     grad_cond = jnp.sum(far_parts.astype(jnp.float32), axis=0)
     return (grad_queries, grad_cond.T.astype(jnp.bfloat16))
 

time: 110 us -> 105 us (0.955)
  blocking collectives: 64.7 us -> 0 us
  starting transfers between devices: 0.04 us -> 40.9 us
  waiting for transfers between devices: 0.02 us -> 20.6 us
  between operations: 14 us -> 0.69 us
  Pallas kernels: 27.5 us -> 36.7 us
  other arithmetic: 1.48 us -> 4.87 us
    all_to_all x3 -> x0, blocking collectives: 64.7 us -> none  [the longest x1 24.2 us: body(): near_parts = lax.all_to_all(grad_c, NEAR, 0, 0, tiled=True)]
    all_to_all x0 -> x3, starting transfers between devices: none -> 26.7 us  [the longest x1 13.7 us: body(): far_parts = lax.all_to_all(near_sum, 'z', 0, 0, tiled=True)]
    ppermute x0 -> x4, starting transfers between devices: none -> 14.2 us  [the longest x3 12.3 us: body(): lax.ppermute(halves[chip], CHIPS, [(i, i ^ chip) for i in range(chips)])]
    all_to_all x0 -> x3, waiting for transfers between devices: none -> 13.7 us  [the longest x1 12.3 us: body(): far_parts = lax.all_to_all(near_sum, 'z', 0, 0, tiled=True)]
    pallas_call x1 -> x2, Pallas kernels: 14.1 us -> 23.1 us  [the longest x1 14.7 us: body(): pl.pallas_call(grads_kernel, grid=(pairs,), in_specs=[pl.BlockSpec(memory...]
    ppermute x0 -> x4, waiting for transfers between devices: none -> 6.9 us  [the longest x3 4.72 us: body(): lax.ppermute(halves[chip], CHIPS, [(i, i ^ chip) for i in range(chips)])]
    convert_element_type x0 -> x2, other arithmetic: none -> 2.82 us  [add(): sum((part.astype(jnp.float32) for part in parts)).astype(jnp.bfloat16)]
  transfers between devices with their start and end apart: 1 -> 7, of which waited for: 0 -> 5; matrix products, arithmetic and copies ran while one was open for 1% -> 4% of each run, Pallas kernels for 0% -> 8%
where the time goes in v2:
time: 105 us; the launch traced here: 104 us
  starting transfers between devices  40.9 us (39%)
  Pallas kernels  36.7 us (35%)
  waiting for transfers between devices  20.6 us (20%)
  other arithmetic  4.87 us (5%)
    pallas_call x1, Pallas kernels, body(): pl.pallas_call(grads_kernel, grid=(pairs,), in_specs=[pl.BlockSpec(memory...  14.7 us
    all_to_all x1, starting transfers between devices, body(): far_parts = lax.all_to_all(near_sum, 'z', 0, 0, tiled=True)  13.7 us
    pallas_call x1, Pallas kernels, body(): pl.pallas_call(scores_kernel, grid=(pairs,), in_specs=[columns(lat_rows),...  13.6 us
    ppermute x3, starting transfers between devices, body(): lax.ppermute(halves[chip], CHIPS, [(i, i ^ chip) for i in range(chips)])  12.3 us
    all_to_all x1, waiting for transfers between devices, body(): far_parts = lax.all_to_all(near_sum, 'z', 0, 0, tiled=True)  12.3 us
    pallas_call x1, Pallas kernels, body(): pl.pallas_call(queries_kernel, grid=(pairs,), in_specs=[columns(cond_rows...  8.42 us
    all_to_all x1, starting transfers between devices, body(): sums = lax.all_to_all(sums, 'date', 0, 0, tiled=True)  7.11 us
    all_to_all x1, starting transfers between devices, body(): lax.all_to_all(grad_q.reshape(dates, lat_rows // dates, local_width), 'da...  5.84 us
  transfers between devices with their start and end apart: 7, of which 5 were waited for; matrix products, arithmetic and copies ran while one was open for 4% of the time, Pallas kernels for 8%

profile of v2, /device:TPU:6, one launch (start us, length us, event | category | flops | bytes accessed | tf_op | source)
XLA Modules:
  0.0 104.3 jit_solution(7627247091909848604)
XLA Ops:
  0.6 13.6 %scores.1 = (bf16[12,384,512]{2,1,0:T(8,128)(2,1)}, bf16[12,384,512]{2,1,0:T(8,128)(2,1)}, bf16[8,6,4,512]{3,2,1,0:T(4,128)(2,1)}, f32[384,768]{1,0:T(8,128)}) custom-call(bf16[512,768]{1,0:T(8,128)(2,1)} %q_ref.3, bf16[512,768]{1,0:T(8,128)(2,1)} %g_ref.3, bf16[384,1536]{1,0:T(8,128)(2,1)} %cond_ref.1, bf16[1536,768]{1,0:T(8,128)(2,1)} %wk_ref.3, ...), custom_call_target="tpu_custom_call" | custom-call | tf_op jit(solution)/shard_map/scores/pallas_call | solution.py:175
  14.2 7.1 %all-to-all-start = ((bf16[8,6,4,512]{3,2,1,0:T(4,128)(2,1)}), bf16[8,6,4,512]{3,2,1,0:T(4,128)(2,1)S(1)}, u32[]{:S(2)}, u32[]{:S(2)}) async-start(bf16[8,6,4,512]{3,2,1,0:T(4,128)(2,1)} %get-tuple-element.18), calls=%async_computation | async-start | bytes 393216 | tf_op jit(solution)/shard_map/all_to_all | solution.py:197
  21.3 8.4 %queries.1 = (f32[12,64,512]{2,1,0:T(8,128)}, f32[12,64,512]{2,1,0:T(8,128)}) custom-call(f32[384,768]{1,0:T(8,128)} %get-tuple-element.13.keys_ref, bf16[12,384,512]{2,1,0:T(8,128)(2,1)} %get-tuple-element.14.w_ref, bf16[12,384,512]{2,1,0:T(8,128)(2,1)} %get-tuple-element.15.e_ref), custom_call_target="tpu_custom_call" | custom-call | tf_op jit(solution)/shard_map/queries/pallas_call | solution.py:198
  29.8 0.7 pad_add_fusion.place_ref
  30.4 1.4 %all-to-all-done.sums_ref = bf16[8,6,4,512]{3,2,1,0:T(4,128)(2,1)S(1)} async-done(((bf16[8,6,4,512]{3,2,1,0:T(4,128)(2,1)}), bf16[8,6,4,512]{3,2,1,0:T(4,128)(2,1)S(1)}, u32[]{:S(2)}, u32[]{:S(2)}) %all-to-all-start) | async-done | bytes 196640 | tf_op jit(solution)/shard_map/all_to_all | solution.py:197
  31.8 0.0 copy-start
  31.8 0.7 copy-done
  32.5 14.7 %grads.1 = (bf16[512,768]{1,0:T(8,128)(2,1)}, bf16[4,12,16,384]{3,2,1,0:T(8,128)(2,1)}, bf16[4,12,16,384]{3,2,1,0:T(8,128)(2,1)}) custom-call(s32[3]{0:T(128)} %pad_add_fusion.place_ref, bf16[512,768]{1,0:T(8,128)(2,1)} %q_ref.3, bf16[512,768]{1,0:T(8,128)(2,1)} %g_ref.3, f32[384,768]{1,0:T(8,128)} %get-tuple-element.13.keys_ref, bf16[1536,768]{1,0:T(8,128)(2,1)} %wk_ref.3, ...), custom_call_target="tpu_custom_call" | custom-call | tf_op jit(solution)/shard_map/grads/pallas_call | solution.py:208
  47.1 5.8 %all-to-all-start.1 = ((bf16[8,64,768]{2,1,0:T(8,128)(2,1)}), bf16[8,64,768]{2,1,0:T(8,128)(2,1)S(1)}, u32[]{:S(2)}, u32[]{:S(2)}) async-start(bf16[8,64,768]{2,1,0:T(8,128)(2,1)} %bitcast.16), calls=%async_computation.1 | async-start | bytes 1572864 | tf_op jit(solution)/shard_map/all_to_all | solution.py:237
  53.0 1.9 %collective-permute-start = (bf16[4,12,16,384]{3,2,1,0:T(8,128)(2,1)}, bf16[4,12,16,384]{3,2,1,0:T(8,128)(2,1)S(1)}, u32[]{:S(2)}, u32[]{:S(2)}) collective-permute-start(bf16[4,12,16,384]{3,2,1,0:T(8,128)(2,1)} %get-tuple-element.20), channel_id=1, source_target_pairs={{0,16},{16,0},{1,17},{17,1},{2,18},{18,2},{3,19},{19,3},{4,20},{20... | collective-permute-start | bytes 1769480 | tf_op jit(solution)/shard_map/ppermute | solution.py:240
  54.9 2.2 %collective-permute-done = bf16[4,12,16,384]{3,2,1,0:T(8,128)(2,1)S(1)} collective-permute-done((bf16[4,12,16,384]{3,2,1,0:T(8,128)(2,1)}, bf16[4,12,16,384]{3,2,1,0:T(8,128)(2,1)S(1)}, u32[]{:S(2)}, u32[]{:S(2)}) %collective-permute-start) | collective-permute-done | bytes 589856 | tf_op jit(solution)/shard_map/ppermute | solution.py:240
  57.1 1.2 %fusion.4 = (bf16[12,16,384]{2,1,0:T(8,128)(2,1)S(1)}, bf16[12,16,384]{2,1,0:T(8,128)(2,1)S(1)}, bf16[12,16,384]{2,1,0:T(8,128)(2,1)S(1)}) fusion(bf16[4,12,16,384]{3,2,1,0:T(8,128)(2,1)S(1)} %collective-permute-done, bf16[4,12,16,384]{3,2,1,0:T(8,128)(2,1)} %get-tuple-element.19), kind=kLoop, calls=%fused_computation.9 | loop fusion | flops 884736 | bytes 1327104 | tf_op jit(solution)/shard_map/convert_element_type | solution.py:155
  58.2 3.3 %collective-permute-start.1 = (bf16[12,16,384]{2,1,0:T(8,128)(2,1)S(1)}, bf16[12,16,384]{2,1,0:T(8,128)(2,1)S(1)}, u32[]{:S(2)}, u32[]{:S(2)}) collective-permute-start(bf16[12,16,384]{2,1,0:T(8,128)(2,1)S(1)} %get-tuple-element.24), channel_id=1, source_target_pairs={{0,1},{1,0},{32,33},{33,32},{2,3},{3,2},{34,35},{35,34},{4,5},{5,4... | collective-permute-start | bytes 442376 | tf_op jit(solution)/shard_map/ppermute | solution.py:243
  61.6 6.2 %collective-permute-start.3 = (bf16[12,16,384]{2,1,0:T(8,128)(2,1)S(1)}, bf16[12,16,384]{2,1,0:T(8,128)(2,1)S(1)}, u32[]{:S(2)}, u32[]{:S(2)}) collective-permute-start(bf16[12,16,384]{2,1,0:T(8,128)(2,1)S(1)} %get-tuple-element.25), channel_id=1, source_target_pairs={{0,33},{1,32},{32,1},{33,0},{2,35},{3,34},{34,3},{35,2},{4,37},{5,... | collective-permute-start | bytes 442376 | tf_op jit(solution)/shard_map/ppermute | solution.py:243
  67.8 2.8 %collective-permute-start.2 = (bf16[12,16,384]{2,1,0:T(8,128)(2,1)S(1)}, bf16[12,16,384]{2,1,0:T(8,128)(2,1)S(1)}, u32[]{:S(2)}, u32[]{:S(2)}) collective-permute-start(bf16[12,16,384]{2,1,0:T(8,128)(2,1)S(1)} %get-tuple-element.26), channel_id=1, source_target_pairs={{0,32},{1,33},{32,0},{33,1},{2,34},{3,35},{34,2},{35,3},{4,36},{5,... | collective-permute-start | bytes 442376 | tf_op jit(solution)/shard_map/ppermute | solution.py:243
  70.6 0.0 collective-permute-done.1
  70.6 2.1 %collective-permute-done.3 = bf16[12,16,384]{2,1,0:T(8,128)(2,1)S(1)} collective-permute-done((bf16[12,16,384]{2,1,0:T(8,128)(2,1)S(1)}, bf16[12,16,384]{2,1,0:T(8,128)(2,1)S(1)}, u32[]{:S(2)}, u32[]{:S(2)}) %collective-permute-start.3) | collective-permute-done | bytes 147488 | tf_op jit(solution)/shard_map/ppermute | solution.py:243
  72.7 2.6 %collective-permute-done.2 = bf16[12,16,384]{2,1,0:T(8,128)(2,1)S(1)} collective-permute-done((bf16[12,16,384]{2,1,0:T(8,128)(2,1)S(1)}, bf16[12,16,384]{2,1,0:T(8,128)(2,1)S(1)}, u32[]{:S(2)}, u32[]{:S(2)}) %collective-permute-start.2) | collective-permute-done | bytes 147488 | tf_op jit(solution)/shard_map/ppermute | solution.py:243
  75.3 1.7 %fusion.2 = bf16[12,16,384]{2,1,0:T(8,128)(2,1)} fusion(bf16[12,16,384]{2,1,0:T(8,128)(2,1)S(1)} %collective-permute-done.3, bf16[12,16,384]{2,1,0:T(8,128)(2,1)S(1)} %collective-permute-done.2, bf16[12,16,384]{2,1,0:T(8,128)(2,1)S(1)} %collective-permute-done.1, bf16[4,12,16,384]{3,2,1,0:T(8,128)(2,1)S(1)} %collective-permute-done, ...), kind=kLoop, calls=%fused_computation.3 | loop fusion | flops 884736 | bytes 884736 | tf_op jit(solution)/shard_map/convert_element_type | solution.py:155
  76.9 0.0 all-to-all-done.1
  76.9 13.7 %all-to-all-start.2 = ((bf16[12,16,384]{2,1,0:T(8,128)(2,1)}), bf16[12,16,384]{2,1,0:T(8,128)(2,1)S(1)}, u32[]{:S(2)}, u32[]{:S(2)}) async-start(bf16[12,16,384]{2,1,0:T(8,128)(2,1)} %fusion.2), calls=%async_computation.2 | async-start | bytes 294912 | tf_op jit(solution)/shard_map/all_to_all | solution.py:247
  90.7 0.8 reduce_sum.24
  91.4 12.3 %all-to-all-done.2 = bf16[12,16,384]{2,1,0:T(8,128)(2,1)S(1)} async-done(((bf16[12,16,384]{2,1,0:T(8,128)(2,1)}), bf16[12,16,384]{2,1,0:T(8,128)(2,1)S(1)}, u32[]{:S(2)}, u32[]{:S(2)}) %all-to-all-start.2) | async-done | bytes 147488 | tf_op jit(solution)/shard_map/all_to_all | solution.py:247
  103.7 0.6 reduce_sum.25
Async XLA Ops:
  14.2 17.6 %all-to-all-start = ((bf16[8,6,4,512]{3,2,1,0:T(4,128)(2,1)}), bf16[8,6,4,512]{3,2,1,0:T(4,128)(2,1)S(1)}, u32[]{:S(2)}, u32[]{:S(2)}) async-start(bf16[8,6,4,512]{3,2,1,0:T(4,128)(2,1)} %get-tuple-element.18), calls=%async_computation | async-start | bytes 393216 | tf_op jit(solution)/shard_map/all_to_all | solution.py:197
  31.8 0.7 copy-start
  47.1 29.8 %all-to-all-start.1 = ((bf16[8,64,768]{2,1,0:T(8,128)(2,1)}), bf16[8,64,768]{2,1,0:T(8,128)(2,1)S(1)}, u32[]{:S(2)}, u32[]{:S(2)}) async-start(bf16[8,64,768]{2,1,0:T(8,128)(2,1)} %bitcast.16), calls=%async_computation.1 | async-start | bytes 1572864 | tf_op jit(solution)/shard_map/all_to_all | solution.py:237
  53.0 4.1 %collective-permute-start = (bf16[4,12,16,384]{3,2,1,0:T(8,128)(2,1)}, bf16[4,12,16,384]{3,2,1,0:T(8,128)(2,1)S(1)}, u32[]{:S(2)}, u32[]{:S(2)}) collective-permute-start(bf16[4,12,16,384]{3,2,1,0:T(8,128)(2,1)} %get-tuple-element.20), channel_id=1, source_target_pairs={{0,16},{16,0},{1,17},{17,1},{2,18},{18,2},{3,19},{19,3},{4,20},{20... | collective-permute-start | bytes 1769480 | tf_op jit(solution)/shard_map/ppermute | solution.py:240
  58.2 12.3 %collective-permute-start.1 = (bf16[12,16,384]{2,1,0:T(8,128)(2,1)S(1)}, bf16[12,16,384]{2,1,0:T(8,128)(2,1)S(1)}, u32[]{:S(2)}, u32[]{:S(2)}) collective-permute-start(bf16[12,16,384]{2,1,0:T(8,128)(2,1)S(1)} %get-tuple-element.24), channel_id=1, source_target_pairs={{0,1},{1,0},{32,33},{33,32},{2,3},{3,2},{34,35},{35,34},{4,5},{5,4... | collective-permute-start | bytes 442376 | tf_op jit(solution)/shard_map/ppermute | solution.py:243
  61.6 11.1 %collective-permute-start.3 = (bf16[12,16,384]{2,1,0:T(8,128)(2,1)S(1)}, bf16[12,16,384]{2,1,0:T(8,128)(2,1)S(1)}, u32[]{:S(2)}, u32[]{:S(2)}) collective-permute-start(bf16[12,16,384]{2,1,0:T(8,128)(2,1)S(1)} %get-tuple-element.25), channel_id=1, source_target_pairs={{0,33},{1,32},{32,1},{33,0},{2,35},{3,34},{34,3},{35,2},{4,37},{5,... | collective-permute-start | bytes 442376 | tf_op jit(solution)/shard_map/ppermute | solution.py:243
  67.8 7.5 %collective-permute-start.2 = (bf16[12,16,384]{2,1,0:T(8,128)(2,1)S(1)}, bf16[12,16,384]{2,1,0:T(8,128)(2,1)S(1)}, u32[]{:S(2)}, u32[]{:S(2)}) collective-permute-start(bf16[12,16,384]{2,1,0:T(8,128)(2,1)S(1)} %get-tuple-element.26), channel_id=1, source_target_pairs={{0,32},{1,33},{32,0},{33,1},{2,34},{3,35},{34,2},{35,3},{4,36},{5,... | collective-permute-start | bytes 442376 | tf_op jit(solution)/shard_map/ppermute | solution.py:243
  76.9 26.8 %all-to-all-start.2 = ((bf16[12,16,384]{2,1,0:T(8,128)(2,1)}), bf16[12,16,384]{2,1,0:T(8,128)(2,1)S(1)}, u32[]{:S(2)}, u32[]{:S(2)}) async-start(bf16[12,16,384]{2,1,0:T(8,128)(2,1)} %fusion.2), calls=%async_computation.2 | async-start | bytes 294912 | tf_op jit(solution)/shard_map/all_to_all | solution.py:247

commit v3 on v2

v3 whole, which is shorter than its diff:
```python
import jax
import jax.numpy as jnp
from jax import lax
from jax.experimental import pallas as pl
from jax.experimental.pallas import tpu as pltpu
from jax.sharding import Mesh, PartitionSpec as P

DH = 64
PAIR = 2 * DH
STEP = 3
SPACE = ("z", "x", "core")
CHIPS = ("x", "head")

NORM_EPSILON = 1e-06

NT = (((1,), (1,)), ((), ()))
NN = (((1,), (0,)), ((), ()))


def dot(a, b, dims=NN):
    return lax.dot_general(a, b, dims, preferred_element_type=jnp.float32)


def head_mean(x):
    first = lax.broadcasted_iota(jnp.int32, x.shape, 1) < DH
    zero = jnp.zeros_like(x)
    left = jnp.sum(jnp.where(first, x, zero), axis=1, keepdims=True)
    right = jnp.sum(jnp.where(first, zero, x), axis=1, keepdims=True)
    return jnp.where(first, left, right) * (1.0 / DH)


def scores_kernel(
    q_ref, g_ref, cond_ref, wk_ref, wv_ref, clear_ref,
    w_ref, e_ref, sums_ref, keys_ref, mask_ref
):
    cond_rows = cond_ref.shape[0]
    lat_rows = q_ref.shape[0]

    @pl.when(pl.program_id(0) == 0)
    def _():
        mask_ref[...] = jnp.broadcast_to(clear_ref[...].astype(jnp.float32), (PAIR, cond_rows)).T

    for sub in range(STEP):
        lanes = slice(sub * PAIR, (sub + 1) * PAIR)
        projected = dot(
            cond_ref[...], jnp.concatenate([wk_ref[:, lanes], wv_ref[:, lanes]], axis=1)
        )
        key_raw = projected[:, :PAIR]
        keys_ref[:, lanes] = key_raw
        key_normed = key_raw * lax.rsqrt(head_mean(key_raw * key_raw) + NORM_EPSILON)
        key_unit = key_normed.astype(jnp.bfloat16)
        values = projected[:, PAIR:].astype(jnp.bfloat16)
        q = q_ref[:, lanes].astype(jnp.float32)
        q_unit = (q * lax.rsqrt(head_mean(q * q) + NORM_EPSILON)).astype(jnp.bfloat16)
        first = lax.broadcasted_iota(jnp.int32, key_unit.shape, 1) < DH
        nothing = jnp.zeros_like(key_unit)
        mask = jnp.concatenate([mask_ref[...]] * (lat_rows // PAIR), axis=1)
        sums = []
        for head in range(2):
            mine = first if head == 0 else ~first
            scores = dot(jnp.where(mine, key_unit, nothing), q_unit, NT) * (DH ** -0.5)
            dprob = dot(jnp.where(mine, values, nothing), g_ref[:, lanes], NT)
            weights = jnp.exp(scores) * mask
            carried = weights * dprob
            w_ref[2 * sub + head] = weights.astype(jnp.bfloat16)
            e_ref[2 * sub + head] = carried.astype(jnp.bfloat16)
            sums += [jnp.sum(weights, axis=0, keepdims=True), jnp.sum(carried, axis=0, keepdims=True)]
        sums = jnp.concatenate(sums, axis=0).astype(sums_ref.dtype)
        sums_ref[:, sub] = jnp.broadcast_to(sums[None], (sums_ref.shape[0],) + sums.shape)


def means_of(sums_ref, pair, head):
    sums = jnp.sum(sums_ref[:, pair, 2 * head : 2 * head + 2].astype(jnp.float32), axis=0)
    inverse = 1.0 / sums[:1]
    return inverse, sums[1:] * inverse


def grads_kernel(
    place_ref, q_ref, g_ref, keys_ref, wk_ref, wv_ref, w_ref, e_ref, sums_ref,
    gq_ref, keep_ref, send_ref, acc_ref
):
    cond_rows = keys_ref.shape[0]
    step = pl.program_id(0)
    both = []
    for sub in range(STEP):
        lanes = slice(sub * PAIR, (sub + 1) * PAIR)
        q = q_ref[:, lanes].astype(jnp.float32)
        q_factor = lax.rsqrt(head_mean(q * q) + NORM_EPSILON)
        q_normed = q * q_factor
        q_unit = q_normed.astype(jnp.bfloat16)
        key_raw = keys_ref[:, lanes]
        key_factor = lax.rsqrt(head_mean(key_raw * key_raw) + NORM_EPSILON)
        key_normed = key_raw * key_factor
        turned = key_normed.T.astype(jnp.bfloat16)
        probs = []
        dscores = []
        for head in range(2):
            inverse, mean = means_of(sums_ref, sub, head)
            weights = w_ref[2 * sub + head].astype(jnp.float32)
            probs.append((weights * inverse).astype(jnp.bfloat16))
            dscore = (e_ref[2 * sub + head].astype(jnp.float32) - weights * mean) * inverse
            dscores.append(dscore.astype(jnp.bfloat16))
        gq = [dot(turned[head * DH : (head + 1) * DH], dscores[head]) for head in range(2)]
        gq = jnp.concatenate(gq, axis=0).T * (DH ** -0.5)
        gq = q_factor * (gq - q_normed * head_mean(gq * q_normed))
        gq_ref[:, lanes] = gq.astype(gq_ref.dtype)
        lane = lax.broadcasted_iota(jnp.int32, (cond_rows, PAIR), 1)
        grad_values = dot(jnp.concatenate(probs, axis=0), g_ref[:, lanes])
        grad_keys = dot(jnp.concatenate(dscores, axis=0), q_unit)
        gv = jnp.where(lane < DH, grad_values[:cond_rows], grad_values[cond_rows:])
        gk = jnp.where(lane < DH, grad_keys[:cond_rows], grad_keys[cond_rows:]) * (DH ** -0.5)
        gk_back = key_factor * (gk - key_normed * head_mean(gk * key_normed))
        both += [gk_back.astype(jnp.bfloat16), gv.astype(jnp.bfloat16)]
    w_both = []
    for sub in range(STEP):
        lanes = slice(sub * PAIR, (sub + 1) * PAIR)
        w_both += [wk_ref[:, lanes], wv_ref[:, lanes]]
    part = dot(jnp.concatenate(w_both, axis=1), jnp.concatenate(both, axis=1), NT)

    @pl.when(step == 0)
    def _():
        acc_ref[...] = part

    @pl.when(step > 0)
    def _():
        acc_ref[...] += part

    @pl.when(step == pl.num_programs(0) - 1)
    def _():
        chips, far, own = keep_ref.shape[:3]
        x, core, head = place_ref[0], place_ref[1], place_ref[2]
        for chip in range(chips):
            to_x = x ^ (chip // 2)
            to_head = head ^ (chip % 2)
            for ref, to_core in ((keep_ref, core), (send_ref, core ^ 1)):
                near = (to_x * 2 + to_core) * 2 + to_head
                for i in range(far):
                    start = pl.multiple_of((i * 8 + near) * own, own)
                    ref[chip, i] = acc_ref[pl.ds(start, own), :].astype(ref.dtype)


def columns(rows):
    return pl.BlockSpec((rows, STEP * PAIR), lambda i: (0, i))


def whole(shape):
    return pl.BlockSpec(shape, lambda i: (0,) * len(shape), pipeline_mode=pl.Buffered(1))


def in_hbm(*arrays):
    return [pltpu.with_memory_space_constraint(array, pltpu.HBM) for array in arrays]


def add(*parts):
    return sum(part.astype(jnp.float32) for part in parts).astype(jnp.bfloat16)


def body(latent_queries, grad_attention, cond_tokens, w_key, w_value, clear_tokens):
    lat_rows, local_width = latent_queries.shape
    cond_rows, width = cond_tokens.shape
    pairs = local_width // PAIR
    latent_queries, grad_attention, cond_tokens, w_key, w_value = in_hbm(
        latent_queries, grad_attention, cond_tokens, w_key, w_value
    )
    dates = lax.axis_size("date")
    far = lax.axis_size("z")
    chips = lax.axis_size(CHIPS)
    own = width // (far * chips * 2)
    params = pltpu.CompilerParams(
        dimension_semantics=("arbitrary",), vmem_limit_bytes=36 * 1024 * 1024
    )
    score_block = pl.BlockSpec((2 * STEP, cond_rows, lat_rows), lambda i: (i, 0, 0))
    sums_block = pl.BlockSpec((dates, STEP, 4, lat_rows), lambda i: (0, i, 0, 0))
    score_shape = pltpu.HBM((2 * pairs, cond_rows, lat_rows), jnp.bfloat16)
    piece_shape = pltpu.HBM((chips, far, own, cond_rows), jnp.bfloat16)
    weights, carried, sums, key_raw = pl.pallas_call(
        scores_kernel,
        grid=(pairs // STEP,),
        in_specs=[
            columns(lat_rows),
            columns(lat_rows),
            whole((cond_rows, width)),
            columns(width),
            columns(width),
            whole((1, cond_rows)),
        ],
        out_specs=[score_block, score_block, sums_block, columns(cond_rows)],
        out_shape=[
            score_shape,
            score_shape,
            pltpu.HBM((dates, pairs, 4, lat_rows), jnp.bfloat16),
            pltpu.HBM((cond_rows, local_width), jnp.float32),
        ],
        scratch_shapes=[pltpu.VMEM((cond_rows, PAIR), jnp.float32)],
        compiler_params=params,
        name="scores",
    )(latent_queries, grad_attention, cond_tokens, w_key, w_value, clear_tokens)
    weights, carried, key_raw = in_hbm(weights, carried, key_raw)
    sums = lax.all_to_all(sums, "date", 0, 0, tiled=True)
    place = jnp.stack([lax.axis_index("x"), lax.axis_index("core"), lax.axis_index("head")])
    grad_q, keep, send = pl.pallas_call(
        grads_kernel,
        grid=(pairs // STEP,),
        in_specs=[
            pl.BlockSpec(memory_space=pltpu.SMEM),
            columns(lat_rows),
            columns(lat_rows),
            columns(cond_rows),
            columns(width),
            columns(width),
            score_block,
            score_block,
            sums_block,
        ],
        out_specs=[columns(lat_rows), whole(piece_shape.shape), whole(piece_shape.shape)],
        out_shape=[
            jax.ShapeDtypeStruct((lat_rows, local_width), jnp.bfloat16),
            piece_shape,
            piece_shape,
        ],
        scratch_shapes=[pltpu.VMEM((width, cond_rows), jnp.float32)],
        compiler_params=params,
        name="grads",
    )(place, latent_queries, grad_attention, key_raw, w_key, w_value, weights, carried, sums)
    share_parts = lax.all_to_all(
        grad_q.reshape(dates, lat_rows // dates, local_width), "date", 0, 0, tiled=True
    )
    other = lax.ppermute(send, "core", [(0, 1), (1, 0)])
    halves = [add(keep[chip], other[chip]) for chip in range(chips)]
    near_parts = halves[:1] + [
        lax.ppermute(halves[chip], CHIPS, [(i, i ^ chip) for i in range(chips)])
        for chip in range(1, chips)
    ]
    near_sum, share_parts = lax.optimization_barrier((add(*near_parts), share_parts))
    far_parts = lax.all_to_all(near_sum, "z", 0, 0, tiled=True)
    grad_queries = jnp.sum(share_parts.astype(jnp.float32), axis=0).astype(jnp.bfloat16)
    grad_cond = jnp.sum(far_parts.astype(jnp.float32), axis=0)
    return (grad_queries, grad_cond.T.astype(jnp.bfloat16))


def solution(mesh):
    space, dates, heads = mesh.devices.shape
    split = Mesh(
        mesh.devices.reshape(space // 4, 2, 2, dates, heads), ("z", "x", "core", "date", "head")
    )
    return jax.shard_map(
        body,
        mesh=split,
        in_specs=(
            P(SPACE, "head"),
            P(SPACE, "head"),
            P("date", None),
            P(None, "head"),
            P(None, "head"),
            P(SPACE, "date"),
        ),
        out_specs=(P(SPACE + ("date",), "head"), P("date", SPACE + ("head",))),
        check_vma=False,
    )
```

time: 105 us -> 97.6 us (0.930)
  Pallas kernels: 36.7 us -> 24.2 us
  waiting for transfers between devices: 20.6 us -> 28.6 us
  starting transfers between devices: 40.9 us -> 37.5 us
    pallas_call x3 -> x2, Pallas kernels: 36.7 us -> 24.2 us  [the longest x1 13 us: body(): pl.pallas_call(grads_kernel, grid=(pairs // STEP,), in_specs=[pl.BlockSpe...]
    all_to_all x1, waiting for transfers between devices: 1.39 us -> 10.4 us  [body(): sums = lax.all_to_all(sums, 'date', 0, 0, tiled=True)]
    all_to_all x1, starting transfers between devices: 5.84 us -> 3.56 us  [body(): lax.all_to_all(grad_q.reshape(dates, lat_rows // dates, local_width), 'da...]
  transfers between devices with their start and end apart: 7 -> 7, of which waited for: 5 -> 5; matrix products, arithmetic and copies ran while one was open for 4% -> 4% of each run, Pallas kernels for 8% -> 0%
where the time goes in v3:
time: 97.6 us; the launch traced here: 96.1 us
  starting transfers between devices  37.5 us (38%)
  waiting for transfers between devices  28.6 us (29%)
  Pallas kernels  24.2 us (25%)
  other arithmetic  4.28 us (4%)
    all_to_all x1, starting transfers between devices, body(): far_parts = lax.all_to_all(near_sum, 'z', 0, 0, tiled=True)  13.4 us
    pallas_call x1, Pallas kernels, body(): pl.pallas_call(grads_kernel, grid=(pairs // STEP,), in_specs=[pl.BlockSpe...  13 us
    ppermute x3, starting transfers between devices, body(): lax.ppermute(halves[chip], CHIPS, [(i, i ^ chip) for i in range(chips)])  11.6 us
    all_to_all x1, waiting for transfers between devices, body(): far_parts = lax.all_to_all(near_sum, 'z', 0, 0, tiled=True)  11.3 us
    pallas_call x1, Pallas kernels, body(): pl.pallas_call(scores_kernel, grid=(pairs // STEP,), in_specs=[columns(la...  11.2 us
    all_to_all x1, waiting for transfers between devices, body(): sums = lax.all_to_all(sums, 'date', 0, 0, tiled=True)  10.4 us
    all_to_all x1, starting transfers between devices, body(): sums = lax.all_to_all(sums, 'date', 0, 0, tiled=True)  7.1 us
    ppermute x3, waiting for transfers between devices, body(): lax.ppermute(halves[chip], CHIPS, [(i, i ^ chip) for i in range(chips)])  4.72 us
  transfers between devices with their start and end apart: 7, of which 5 were waited for; matrix products, arithmetic and copies ran while one was open for 4% of the time, Pallas kernels for 0%

profile of v3, /device:TPU:6, one launch (start us, length us, event | category | flops | bytes accessed | tf_op | source)
XLA Modules:
  0.0 96.1 jit_solution(17178765234547241311)
XLA Ops:
  0.6 0.0 copy-start
  0.6 0.7 copy-done
  1.3 11.2 %scores.1 = (bf16[12,384,512]{2,1,0:T(8,128)(2,1)}, bf16[12,384,512]{2,1,0:T(8,128)(2,1)}, bf16[8,6,4,512]{3,2,1,0:T(4,128)(2,1)}, f32[384,768]{1,0:T(8,128)}) custom-call(bf16[512,768]{1,0:T(8,128)(2,1)} %q_ref.3, bf16[512,768]{1,0:T(8,128)(2,1)} %g_ref.3, bf16[384,1536]{1,0:T(8,128)(2,1)} %cond_ref.1, bf16[1536,768]{1,0:T(8,128)(2,1)} %wk_ref.3, ...), custom_call_target="tpu_custom_call" | custom-call | tf_op jit(solution)/shard_map/scores/pallas_call | solution.py:176
  12.5 7.1 %all-to-all-start = ((bf16[8,6,4,512]{3,2,1,0:T(4,128)(2,1)}), bf16[8,6,4,512]{3,2,1,0:T(4,128)(2,1)S(1)}, u32[]{:S(2)}, u32[]{:S(2)}) async-start(bf16[8,6,4,512]{3,2,1,0:T(4,128)(2,1)} %get-tuple-element.14), calls=%async_computation | async-start | bytes 393216 | tf_op jit(solution)/shard_map/all_to_all | solution.py:199
  19.6 0.1 pad_add_fusion.place_ref
  19.7 10.4 %all-to-all-done.sums_ref = bf16[8,6,4,512]{3,2,1,0:T(4,128)(2,1)S(1)} async-done(((bf16[8,6,4,512]{3,2,1,0:T(4,128)(2,1)}), bf16[8,6,4,512]{3,2,1,0:T(4,128)(2,1)S(1)}, u32[]{:S(2)}, u32[]{:S(2)}) %all-to-all-start) | async-done | bytes 196640 | tf_op jit(solution)/shard_map/all_to_all | solution.py:199
  30.1 13.0 %grads.1 = (bf16[512,768]{1,0:T(8,128)(2,1)}, bf16[4,12,16,384]{3,2,1,0:T(8,128)(2,1)}, bf16[4,12,16,384]{3,2,1,0:T(8,128)(2,1)}) custom-call(s32[3]{0:T(128)S(1)} %pad_add_fusion.place_ref, bf16[512,768]{1,0:T(8,128)(2,1)} %q_ref.3, bf16[512,768]{1,0:T(8,128)(2,1)} %g_ref.3, f32[384,768]{1,0:T(8,128)} %get-tuple-element.11.keys_ref, ...), custom_call_target="tpu_custom_call" | custom-call | tf_op jit(solution)/shard_map/grads/pallas_call | solution.py:201
  43.1 3.6 %all-to-all-start.1 = ((bf16[8,64,768]{2,1,0:T(8,128)(2,1)}), bf16[8,64,768]{2,1,0:T(8,128)(2,1)S(1)}, u32[]{:S(2)}, u32[]{:S(2)}) async-start(bf16[8,64,768]{2,1,0:T(8,128)(2,1)} %bitcast.7), calls=%async_computation.1 | async-start | bytes 1572864 | tf_op jit(solution)/shard_map/all_to_all | solution.py:225
  46.7 1.9 %collective-permute-start = (bf16[4,12,16,384]{3,2,1,0:T(8,128)(2,1)}, bf16[4,12,16,384]{3,2,1,0:T(8,128)(2,1)S(1)}, u32[]{:S(2)}, u32[]{:S(2)}) collective-permute-start(bf16[4,12,16,384]{3,2,1,0:T(8,128)(2,1)} %get-tuple-element.16), channel_id=1, source_target_pairs={{0,16},{16,0},{1,17},{17,1},{2,18},{18,2},{3,19},{19,3},{4,20},{20... | collective-permute-start | bytes 1769480 | tf_op jit(solution)/shard_map/ppermute | solution.py:228
  48.6 2.2 %collective-permute-done = bf16[4,12,16,384]{3,2,1,0:T(8,128)(2,1)S(1)} collective-permute-done((bf16[4,12,16,384]{3,2,1,0:T(8,128)(2,1)}, bf16[4,12,16,384]{3,2,1,0:T(8,128)(2,1)S(1)}, u32[]{:S(2)}, u32[]{:S(2)}) %collective-permute-start) | collective-permute-done | bytes 589856 | tf_op jit(solution)/shard_map/ppermute | solution.py:228
  50.8 1.2 %fusion.4 = (bf16[12,16,384]{2,1,0:T(8,128)(2,1)S(1)}, bf16[12,16,384]{2,1,0:T(8,128)(2,1)S(1)}, bf16[12,16,384]{2,1,0:T(8,128)(2,1)S(1)}) fusion(bf16[4,12,16,384]{3,2,1,0:T(8,128)(2,1)S(1)} %collective-permute-done, bf16[4,12,16,384]{3,2,1,0:T(8,128)(2,1)} %get-tuple-element.15), kind=kLoop, calls=%fused_computation.9 | loop fusion | flops 884736 | bytes 1327104 | tf_op jit(solution)/shard_map/convert_element_type | solution.py:155
  52.0 3.3 %collective-permute-start.1 = (bf16[12,16,384]{2,1,0:T(8,128)(2,1)S(1)}, bf16[12,16,384]{2,1,0:T(8,128)(2,1)S(1)}, u32[]{:S(2)}, u32[]{:S(2)}) collective-permute-start(bf16[12,16,384]{2,1,0:T(8,128)(2,1)S(1)} %get-tuple-element.20), channel_id=1, source_target_pairs={{0,1},{1,0},{32,33},{33,32},{2,3},{3,2},{34,35},{35,34},{4,5},{5,4... | collective-permute-start | bytes 442376 | tf_op jit(solution)/shard_map/ppermute | solution.py:231
  55.3 5.5 %collective-permute-start.3 = (bf16[12,16,384]{2,1,0:T(8,128)(2,1)S(1)}, bf16[12,16,384]{2,1,0:T(8,128)(2,1)S(1)}, u32[]{:S(2)}, u32[]{:S(2)}) collective-permute-start(bf16[12,16,384]{2,1,0:T(8,128)(2,1)S(1)} %get-tuple-element.21), channel_id=1, source_target_pairs={{0,33},{1,32},{32,1},{33,0},{2,35},{3,34},{34,3},{35,2},{4,37},{5,... | collective-permute-start | bytes 442376 | tf_op jit(solution)/shard_map/ppermute | solution.py:231
  60.8 2.8 %collective-permute-start.2 = (bf16[12,16,384]{2,1,0:T(8,128)(2,1)S(1)}, bf16[12,16,384]{2,1,0:T(8,128)(2,1)S(1)}, u32[]{:S(2)}, u32[]{:S(2)}) collective-permute-start(bf16[12,16,384]{2,1,0:T(8,128)(2,1)S(1)} %get-tuple-element.22), channel_id=1, source_target_pairs={{0,32},{1,33},{32,0},{33,1},{2,34},{3,35},{34,2},{35,3},{4,36},{5,... | collective-permute-start | bytes 442376 | tf_op jit(solution)/shard_map/ppermute | solution.py:231
  63.6 0.0 collective-permute-done.1
  63.6 2.1 %collective-permute-done.3 = bf16[12,16,384]{2,1,0:T(8,128)(2,1)S(1)} collective-permute-done((bf16[12,16,384]{2,1,0:T(8,128)(2,1)S(1)}, bf16[12,16,384]{2,1,0:T(8,128)(2,1)S(1)}, u32[]{:S(2)}, u32[]{:S(2)}) %collective-permute-start.3) | collective-permute-done | bytes 147488 | tf_op jit(solution)/shard_map/ppermute | solution.py:231
  65.7 2.6 %collective-permute-done.2 = bf16[12,16,384]{2,1,0:T(8,128)(2,1)S(1)} collective-permute-done((bf16[12,16,384]{2,1,0:T(8,128)(2,1)S(1)}, bf16[12,16,384]{2,1,0:T(8,128)(2,1)S(1)}, u32[]{:S(2)}, u32[]{:S(2)}) %collective-permute-start.2) | collective-permute-done | bytes 147488 | tf_op jit(solution)/shard_map/ppermute | solution.py:231
  68.3 1.7 %fusion.2 = bf16[12,16,384]{2,1,0:T(8,128)(2,1)} fusion(bf16[12,16,384]{2,1,0:T(8,128)(2,1)S(1)} %collective-permute-done.3, bf16[12,16,384]{2,1,0:T(8,128)(2,1)S(1)} %collective-permute-done.2, bf16[12,16,384]{2,1,0:T(8,128)(2,1)S(1)} %collective-permute-done.1, bf16[4,12,16,384]{3,2,1,0:T(8,128)(2,1)S(1)} %collective-permute-done, ...), kind=kLoop, calls=%fused_computation.3 | loop fusion | flops 884736 | bytes 884736 | tf_op jit(solution)/shard_map/convert_element_type | solution.py:155
  70.0 0.0 all-to-all-done.1
  70.0 13.4 %all-to-all-start.2 = ((bf16[12,16,384]{2,1,0:T(8,128)(2,1)}), bf16[12,16,384]{2,1,0:T(8,128)(2,1)S(1)}, u32[]{:S(2)}, u32[]{:S(2)}) async-start(bf16[12,16,384]{2,1,0:T(8,128)(2,1)} %fusion.2), calls=%async_computation.2 | async-start | bytes 294912 | tf_op jit(solution)/shard_map/all_to_all | solution.py:235
  83.4 0.8 reduce_sum.24
  84.1 11.3 %all-to-all-done.2 = bf16[12,16,384]{2,1,0:T(8,128)(2,1)S(1)} async-done(((bf16[12,16,384]{2,1,0:T(8,128)(2,1)}), bf16[12,16,384]{2,1,0:T(8,128)(2,1)S(1)}, u32[]{:S(2)}, u32[]{:S(2)}) %all-to-all-start.2) | async-done | bytes 147488 | tf_op jit(solution)/shard_map/all_to_all | solution.py:235
  95.5 0.6 reduce_sum.25
Async XLA Ops:
  0.6 0.7 copy-start
  12.5 17.6 %all-to-all-start = ((bf16[8,6,4,512]{3,2,1,0:T(4,128)(2,1)}), bf16[8,6,4,512]{3,2,1,0:T(4,128)(2,1)S(1)}, u32[]{:S(2)}, u32[]{:S(2)}) async-start(bf16[8,6,4,512]{3,2,1,0:T(4,128)(2,1)} %get-tuple-element.14), calls=%async_computation | async-start | bytes 393216 | tf_op jit(solution)/shard_map/all_to_all | solution.py:199
  43.1 26.9 %all-to-all-start.1 = ((bf16[8,64,768]{2,1,0:T(8,128)(2,1)}), bf16[8,64,768]{2,1,0:T(8,128)(2,1)S(1)}, u32[]{:S(2)}, u32[]{:S(2)}) async-start(bf16[8,64,768]{2,1,0:T(8,128)(2,1)} %bitcast.7), calls=%async_computation.1 | async-start | bytes 1572864 | tf_op jit(solution)/shard_map/all_to_all | solution.py:225
  46.7 4.1 %collective-permute-start = (bf16[4,12,16,384]{3,2,1,0:T(8,128)(2,1)}, bf16[4,12,16,384]{3,2,1,0:T(8,128)(2,1)S(1)}, u32[]{:S(2)}, u32[]{:S(2)}) collective-permute-start(bf16[4,12,16,384]{3,2,1,0:T(8,128)(2,1)} %get-tuple-element.16), channel_id=1, source_target_pairs={{0,16},{16,0},{1,17},{17,1},{2,18},{18,2},{3,19},{19,3},{4,20},{20... | collective-permute-start | bytes 1769480 | tf_op jit(solution)/shard_map/ppermute | solution.py:228
  52.0 11.6 %collective-permute-start.1 = (bf16[12,16,384]{2,1,0:T(8,128)(2,1)S(1)}, bf16[12,16,384]{2,1,0:T(8,128)(2,1)S(1)}, u32[]{:S(2)}, u32[]{:S(2)}) collective-permute-start(bf16[12,16,384]{2,1,0:T(8,128)(2,1)S(1)} %get-tuple-element.20), channel_id=1, source_target_pairs={{0,1},{1,0},{32,33},{33,32},{2,3},{3,2},{34,35},{35,34},{4,5},{5,4... | collective-permute-start | bytes 442376 | tf_op jit(solution)/shard_map/ppermute | solution.py:231
  55.3 10.4 %collective-permute-start.3 = (bf16[12,16,384]{2,1,0:T(8,128)(2,1)S(1)}, bf16[12,16,384]{2,1,0:T(8,128)(2,1)S(1)}, u32[]{:S(2)}, u32[]{:S(2)}) collective-permute-start(bf16[12,16,384]{2,1,0:T(8,128)(2,1)S(1)} %get-tuple-element.21), channel_id=1, source_target_pairs={{0,33},{1,32},{32,1},{33,0},{2,35},{3,34},{34,3},{35,2},{4,37},{5,... | collective-permute-start | bytes 442376 | tf_op jit(solution)/shard_map/ppermute | solution.py:231
  60.8 7.5 %collective-permute-start.2 = (bf16[12,16,384]{2,1,0:T(8,128)(2,1)S(1)}, bf16[12,16,384]{2,1,0:T(8,128)(2,1)S(1)}, u32[]{:S(2)}, u32[]{:S(2)}) collective-permute-start(bf16[12,16,384]{2,1,0:T(8,128)(2,1)S(1)} %get-tuple-element.22), channel_id=1, source_target_pairs={{0,32},{1,33},{32,0},{33,1},{2,34},{3,35},{34,2},{35,3},{4,36},{5,... | collective-permute-start | bytes 442376 | tf_op jit(solution)/shard_map/ppermute | solution.py:231
  70.0 25.5 %all-to-all-start.2 = ((bf16[12,16,384]{2,1,0:T(8,128)(2,1)}), bf16[12,16,384]{2,1,0:T(8,128)(2,1)S(1)}, u32[]{:S(2)}, u32[]{:S(2)}) async-start(bf16[12,16,384]{2,1,0:T(8,128)(2,1)} %fusion.2), calls=%async_computation.2 | async-start | bytes 294912 | tf_op jit(solution)/shard_map/all_to_all | solution.py:235

commit v4 on v3

--- a/solution.py
+++ b/solution.py
@@ -29,9 +29,15 @@
     return jnp.where(first, left, right) * (1.0 / DH)
 
 
+def place_of(sub, head, w_ref, e_ref, w_near_ref, e_near_ref):
+    if sub < STEP - 1:
+        return w_ref, e_ref, 2 * sub + head
+    return w_near_ref, e_near_ref, 2 * pl.program_id(0) + head
+
+
 def scores_kernel(
     q_ref, g_ref, cond_ref, wk_ref, wv_ref, clear_ref,
-    w_ref, e_ref, sums_ref, keys_ref, mask_ref
+    w_ref, e_ref, w_near_ref, e_near_ref, sums_ref, keys_ref, mask_ref
 ):
     cond_rows = cond_ref.shape[0]
     lat_rows = q_ref.shape[0]
@@ -62,8 +68,9 @@
             dprob = dot(jnp.where(mine, values, nothing), g_ref[:, lanes], NT)
             weights = jnp.exp(scores) * mask
             carried = weights * dprob
-            w_ref[2 * sub + head] = weights.astype(jnp.bfloat16)
-            e_ref[2 * sub + head] = carried.astype(jnp.bfloat16)
+            own_w, own_e, at = place_of(sub, head, w_ref, e_ref, w_near_ref, e_near_ref)
+            own_w[at] = weights.astype(jnp.bfloat16)
+            own_e[at] = carried.astype(jnp.bfloat16)
             sums += [jnp.sum(weights, axis=0, keepdims=True), jnp.sum(carried, axis=0, keepdims=True)]
         sums = jnp.concatenate(sums, axis=0).astype(sums_ref.dtype)
         sums_ref[:, sub] = jnp.broadcast_to(sums[None], (sums_ref.shape[0],) + sums.shape)
@@ -76,7 +83,7 @@
 
 
 def grads_kernel(
-    place_ref, q_ref, g_ref, keys_ref, wk_ref, wv_ref, w_ref, e_ref, sums_ref,
+    place_ref, q_ref, g_ref, keys_ref, wk_ref, wv_ref, w_ref, e_ref, w_near_ref, e_near_ref, sums_ref,
     gq_ref, keep_ref, send_ref, acc_ref
 ):
     cond_rows = keys_ref.shape[0]
@@ -96,14 +103,15 @@
         dscores = []
         for head in range(2):
             inverse, mean = means_of(sums_ref, sub, head)
-            weights = w_ref[2 * sub + head].astype(jnp.float32)
+            own_w, own_e, at = place_of(sub, head, w_ref, e_ref, w_near_ref, e_near_ref)
+            weights = own_w[at].astype(jnp.float32)
             probs.append((weights * inverse).astype(jnp.bfloat16))
-            dscore = (e_ref[2 * sub + head].astype(jnp.float32) - weights * mean) * inverse
+            dscore = (own_e[at].astype(jnp.float32) - weights * mean) * inverse
             dscores.append(dscore.astype(jnp.bfloat16))
         gq = [dot(turned[head * DH : (head + 1) * DH], dscores[head]) for head in range(2)]
         gq = jnp.concatenate(gq, axis=0).T * (DH ** -0.5)
         gq = q_factor * (gq - q_normed * head_mean(gq * q_normed))
-        gq_ref[:, lanes] = gq.astype(gq_ref.dtype)
+        gq_ref[:, :, lanes] = gq.astype(gq_ref.dtype).reshape(gq_ref.shape[:2] + (PAIR,))
         lane = lax.broadcasted_iota(jnp.int32, (cond_rows, PAIR), 1)
         grad_values = dot(jnp.concatenate(probs, axis=0), g_ref[:, lanes])
         grad_keys = dot(jnp.concatenate(dscores, axis=0), q_unit)
@@ -159,8 +167,8 @@
     lat_rows, local_width = latent_queries.shape
     cond_rows, width = cond_tokens.shape
     pairs = local_width // PAIR
-    latent_queries, grad_attention, cond_tokens, w_key, w_value = in_hbm(
-        latent_queries, grad_attention, cond_tokens, w_key, w_value
+    latent_queries, grad_attention, cond_tokens, w_key, w_value, clear_tokens = in_hbm(
+        latent_queries, grad_attention, cond_tokens, w_key, w_value, clear_tokens
     )
     dates = lax.axis_size("date")
     far = lax.axis_size("z")
@@ -169,11 +177,14 @@
     params = pltpu.CompilerParams(
         dimension_semantics=("arbitrary",), vmem_limit_bytes=36 * 1024 * 1024
     )
-    score_block = pl.BlockSpec((2 * STEP, cond_rows, lat_rows), lambda i: (i, 0, 0))
+    score_block = pl.BlockSpec((2 * STEP - 2, cond_rows, lat_rows), lambda i: (i, 0, 0))
+    share_block = pl.BlockSpec((dates, lat_rows // dates, STEP * PAIR), lambda i: (0, 0, i))
     sums_block = pl.BlockSpec((dates, STEP, 4, lat_rows), lambda i: (0, i, 0, 0))
-    score_shape = pltpu.HBM((2 * pairs, cond_rows, lat_rows), jnp.bfloat16)
+    score_shape = pltpu.HBM((2 * (pairs - pairs // STEP), cond_rows, lat_rows), jnp.bfloat16)
+    near_shape = pltpu.VMEM((2 * (pairs // STEP), cond_rows, lat_rows), jnp.bfloat16)
+    vmem = pl.BlockSpec(memory_space=pltpu.VMEM)
     piece_shape = pltpu.HBM((chips, far, own, cond_rows), jnp.bfloat16)
-    weights, carried, sums, key_raw = pl.pallas_call(
+    weights, carried, near_weights, near_carried, sums, key_raw = pl.pallas_call(
         scores_kernel,
         grid=(pairs // STEP,),
         in_specs=[
@@ -184,10 +195,12 @@
             columns(width),
             whole((1, cond_rows)),
         ],
-        out_specs=[score_block, score_block, sums_block, columns(cond_rows)],
+        out_specs=[score_block, score_block, vmem, vmem, sums_block, columns(cond_rows)],
         out_shape=[
             score_shape,
             score_shape,
+            near_shape,
+            near_shape,
             pltpu.HBM((dates, pairs, 4, lat_rows), jnp.bfloat16),
             pltpu.HBM((cond_rows, local_width), jnp.float32),
         ],
@@ -210,23 +223,23 @@
             columns(width),
             score_block,
             score_block,
+            vmem,
+            vmem,
             sums_block,
         ],
-        out_specs=[columns(lat_rows), whole(piece_shape.shape), whole(piece_shape.shape)],
+        out_specs=[share_block, whole(piece_shape.shape), whole(piece_shape.shape)],
         out_shape=[
-            jax.ShapeDtypeStruct((lat_rows, local_width), jnp.bfloat16),
+            pltpu.HBM((dates, lat_rows // dates, local_width), jnp.bfloat16),
             piece_shape,
             piece_shape,
         ],
         scratch_shapes=[pltpu.VMEM((width, cond_rows), jnp.float32)],
         compiler_params=params,
         name="grads",
-    )(place, latent_queries, grad_attention, key_raw, w_key, w_value, weights, carried, sums)
-    share_parts = lax.all_to_all(
-        grad_q.reshape(dates, lat_rows // dates, local_width), "date", 0, 0, tiled=True
-    )
+    )(place, latent_queries, grad_attention, key_raw, w_key, w_value, weights, carried, near_weights, near_carried, sums)
+    share_parts = lax.all_to_all(grad_q, "date", 0, 0, tiled=True)
     other = lax.ppermute(send, "core", [(0, 1), (1, 0)])
-    halves = [add(keep[chip], other[chip]) for chip in range(chips)]
+    halves = lax.optimization_barrier([add(keep[chip], other[chip]) for chip in range(chips)])
     near_parts = halves[:1] + [
         lax.ppermute(halves[chip], CHIPS, [(i, i ^ chip) for i in range(chips)])
         for chip in range(1, chips)

time: 97.6 us -> 95.6 us (0.980)
  waiting for transfers between devices: 28.6 us -> 30.1 us
  Pallas kernels: 24.2 us -> 23.1 us
  starting transfers between devices: 37.5 us -> 36.5 us
    ppermute x3, waiting for transfers between devices: 4.72 us -> 6.5 us  [body(): lax.ppermute(halves[chip], CHIPS, [(i, i ^ chip) for i in range(chips)])]
    all_to_all x1, starting transfers between devices: 13.4 us -> 12.3 us  [body(): far_parts = lax.all_to_all(near_sum, 'z', 0, 0, tiled=True)]
  transfers between devices with their start and end apart: 7 -> 7, of which waited for: 5 -> 5; matrix products, arithmetic and copies ran while one was open for 4% -> 3% of each run, Pallas kernels for 0% -> 0%
where the time goes in v4:
time: 95.6 us; the launch traced here: 93.9 us
  starting transfers between devices  36.5 us (38%)
  waiting for transfers between devices  30.1 us (31%)
  Pallas kernels  23.1 us (24%)
  other arithmetic  3.46 us (4%)
    pallas_call x1, Pallas kernels, body(): pl.pallas_call(grads_kernel, grid=(pairs // STEP,), in_specs=[pl.BlockSpe...  12.6 us
    all_to_all x1, starting transfers between devices, body(): far_parts = lax.all_to_all(near_sum, 'z', 0, 0, tiled=True)  12.3 us
    ppermute x3, starting transfers between devices, body(): lax.ppermute(halves[chip], CHIPS, [(i, i ^ chip) for i in range(chips)])  11.6 us
    all_to_all x1, waiting for transfers between devices, body(): far_parts = lax.all_to_all(near_sum, 'z', 0, 0, tiled=True)  11.1 us
    pallas_call x1, Pallas kernels, body(): pl.pallas_call(scores_kernel, grid=(pairs // STEP,), in_specs=[columns(la...  10.6 us
    all_to_all x1, waiting for transfers between devices, body(): sums = lax.all_to_all(sums, 'date', 0, 0, tiled=True)  10.4 us
    all_to_all x1, starting transfers between devices, body(): sums = lax.all_to_all(sums, 'date', 0, 0, tiled=True)  7.1 us
    ppermute x3, waiting for transfers between devices, body(): lax.ppermute(halves[chip], CHIPS, [(i, i ^ chip) for i in range(chips)])  6.5 us
  transfers between devices with their start and end apart: 7, of which 5 were waited for; matrix products, arithmetic and copies ran while one was open for 3% of the time, Pallas kernels for 0%

profile of v4, /device:TPU:6, one launch (start us, length us, event | category | flops | bytes accessed | tf_op | source)
XLA Modules:
  0.0 93.9 jit_solution(5123111982955646429)
XLA Ops:
  0.6 10.6 %scores.1 = (bf16[8,384,512]{2,1,0:T(8,128)(2,1)}, bf16[8,384,512]{2,1,0:T(8,128)(2,1)}, bf16[4,384,512]{2,1,0:T(8,128)(2,1)S(1)}, bf16[4,384,512]{2,1,0:T(8,128...) custom-call(bf16[512,768]{1,0:T(8,128)(2,1)} %q_ref.3, bf16[512,768]{1,0:T(8,128)(2,1)} %g_ref.3, ...), custom_call_target="tpu_custom_call" | custom-call | tf_op jit(solution)/shard_map/scores/pallas_call | solution.py:187
  11.2 7.1 %all-to-all-start = ((bf16[8,6,4,512]{3,2,1,0:T(4,128)(2,1)}), bf16[8,6,4,512]{3,2,1,0:T(4,128)(2,1)S(1)}, u32[]{:S(2)}, u32[]{:S(2)}) async-start(bf16[8,6,4,512]{3,2,1,0:T(4,128)(2,1)} %get-tuple-element.22), calls=%async_computation | async-start | bytes 393216 | tf_op jit(solution)/shard_map/all_to_all | solution.py:212
  18.3 0.1 pad_add_fusion.place_ref
  18.4 10.4 %all-to-all-done.sums_ref = bf16[8,6,4,512]{3,2,1,0:T(4,128)(2,1)S(1)} async-done(((bf16[8,6,4,512]{3,2,1,0:T(4,128)(2,1)}), bf16[8,6,4,512]{3,2,1,0:T(4,128)(2,1)S(1)}, u32[]{:S(2)}, u32[]{:S(2)}) %all-to-all-start) | async-done | bytes 196640 | tf_op jit(solution)/shard_map/all_to_all | solution.py:212
  28.8 12.6 %grads.1 = (bf16[8,64,768]{2,1,0:T(8,128)(2,1)}, bf16[4,12,16,384]{3,2,1,0:T(8,128)(2,1)}, bf16[4,12,16,384]{3,2,1,0:T(8,128)(2,1)}) custom-call(s32[3]{0:T(128)S(1)} %pad_add_fusion.place_ref, bf16[512,768]{1,0:T(8,128)(2,1)} %q_ref.3, bf16[512,768]{1,0:T(8,128)(2,1)} %g_ref.3, f32[384,768]{1,0:T(8,128)} %get-tuple-element.17.keys_ref, ...), custom_call_target="tpu_custom_call" | custom-call | tf_op jit(solution)/shard_map/grads/pallas_call | solution.py:214
  41.3 3.6 %all-to-all-start.1 = ((bf16[8,64,768]{2,1,0:T(8,128)(2,1)}), bf16[8,64,768]{2,1,0:T(8,128)(2,1)S(1)}, u32[]{:S(2)}, u32[]{:S(2)}) async-start(bf16[8,64,768]{2,1,0:T(8,128)(2,1)} %get-tuple-element.29), calls=%async_computation.1 | async-start | bytes 1572864 | tf_op jit(solution)/shard_map/all_to_all | solution.py:240
  44.9 1.9 %collective-permute-start = (bf16[4,12,16,384]{3,2,1,0:T(8,128)(2,1)}, bf16[4,12,16,384]{3,2,1,0:T(8,128)(2,1)S(1)}, u32[]{:S(2)}, u32[]{:S(2)}) collective-permute-start(bf16[4,12,16,384]{3,2,1,0:T(8,128)(2,1)} %get-tuple-element.24), channel_id=1, source_target_pairs={{0,16},{16,0},{1,17},{17,1},{2,18},{18,2},{3,19},{19,3},{4,20},{20... | collective-permute-start | bytes 1769480 | tf_op jit(solution)/shard_map/ppermute | solution.py:241
  46.8 2.2 %collective-permute-done = bf16[4,12,16,384]{3,2,1,0:T(8,128)(2,1)S(1)} collective-permute-done((bf16[4,12,16,384]{3,2,1,0:T(8,128)(2,1)}, bf16[4,12,16,384]{3,2,1,0:T(8,128)(2,1)S(1)}, u32[]{:S(2)}, u32[]{:S(2)}) %collective-permute-start) | collective-permute-done | bytes 589856 | tf_op jit(solution)/shard_map/ppermute | solution.py:241
  49.0 1.3 %fusion.3 = (bf16[12,16,384]{2,1,0:T(8,128)(2,1)S(1)}, bf16[12,16,384]{2,1,0:T(8,128)(2,1)S(1)}, bf16[12,16,384]{2,1,0:T(8,128)(2,1)S(1)}, bf16[12,16,384]{2,1,0:T(8,128)(2,1)S(1)}) fusion(bf16[4,12,16,384]{3,2,1,0:T(8,128)(2,1)S(1)} %collective-permute-done, bf16[4,12,16,384]{3,2,1,0:T(8,128)(2,1)} %get-tuple-element.23), kind=kLoop, calls=%fused_computation.8 | loop fusion | flops 1179648 | bytes 1769472 | tf_op jit(solution)/shard_map/convert_element_type | solution.py:163
  50.3 3.3 %collective-permute-start.1 = (bf16[12,16,384]{2,1,0:T(8,128)(2,1)S(1)}, bf16[12,16,384]{2,1,0:T(8,128)(2,1)S(1)}, u32[]{:S(2)}, u32[]{:S(2)}) collective-permute-start(bf16[12,16,384]{2,1,0:T(8,128)(2,1)S(1)} %get-tuple-element.26), channel_id=1, source_target_pairs={{0,1},{1,0},{32,33},{33,32},{2,3},{3,2},{34,35},{35,34},{4,5},{5,4... | collective-permute-start | bytes 442376 | tf_op jit(solution)/shard_map/ppermute | solution.py:244
  53.6 6.4 %collective-permute-start.2 = (bf16[12,16,384]{2,1,0:T(8,128)(2,1)S(1)}, bf16[12,16,384]{2,1,0:T(8,128)(2,1)S(1)}, u32[]{:S(2)}, u32[]{:S(2)}) collective-permute-start(bf16[12,16,384]{2,1,0:T(8,128)(2,1)S(1)} %get-tuple-element.27), channel_id=1, source_target_pairs={{0,32},{1,33},{32,0},{33,1},{2,34},{3,35},{34,2},{35,3},{4,36},{5,... | collective-permute-start | bytes 442376 | tf_op jit(solution)/shard_map/ppermute | solution.py:244
  60.0 1.9 %collective-permute-start.3 = (bf16[12,16,384]{2,1,0:T(8,128)(2,1)S(1)}, bf16[12,16,384]{2,1,0:T(8,128)(2,1)S(1)}, u32[]{:S(2)}, u32[]{:S(2)}) collective-permute-start(bf16[12,16,384]{2,1,0:T(8,128)(2,1)S(1)} %get-tuple-element.28), channel_id=1, source_target_pairs={{0,33},{1,32},{32,1},{33,0},{2,35},{3,34},{34,3},{35,2},{4,37},{5,... | collective-permute-start | bytes 442376 | tf_op jit(solution)/shard_map/ppermute | solution.py:244
  61.9 0.0 collective-permute-done.1
  61.9 3.1 %collective-permute-done.2 = bf16[12,16,384]{2,1,0:T(8,128)(2,1)S(1)} collective-permute-done((bf16[12,16,384]{2,1,0:T(8,128)(2,1)S(1)}, bf16[12,16,384]{2,1,0:T(8,128)(2,1)S(1)}, u32[]{:S(2)}, u32[]{:S(2)}) %collective-permute-start.2) | collective-permute-done | bytes 147488 | tf_op jit(solution)/shard_map/ppermute | solution.py:244
  65.1 3.3 %collective-permute-done.3 = bf16[12,16,384]{2,1,0:T(8,128)(2,1)S(1)} collective-permute-done((bf16[12,16,384]{2,1,0:T(8,128)(2,1)S(1)}, bf16[12,16,384]{2,1,0:T(8,128)(2,1)S(1)}, u32[]{:S(2)}, u32[]{:S(2)}) %collective-permute-start.3) | collective-permute-done | bytes 147488 | tf_op jit(solution)/shard_map/ppermute | solution.py:244
  68.4 0.7 add_convert_fusion
  69.1 0.0 all-to-all-done.1
  69.2 12.3 %all-to-all-start.2 = ((bf16[12,16,384]{2,1,0:T(8,128)(2,1)}), bf16[12,16,384]{2,1,0:T(8,128)(2,1)S(1)}, u32[]{:S(2)}, u32[]{:S(2)}) async-start(bf16[12,16,384]{2,1,0:T(8,128)(2,1)} %add_convert_fusion), calls=%async_computation.2 | async-start | bytes 294912 | tf_op jit(solution)/shard_map/all_to_all | solution.py:248
  81.5 0.8 reduce_sum.24
  82.2 11.1 %all-to-all-done.2 = bf16[12,16,384]{2,1,0:T(8,128)(2,1)S(1)} async-done(((bf16[12,16,384]{2,1,0:T(8,128)(2,1)}), bf16[12,16,384]{2,1,0:T(8,128)(2,1)S(1)}, u32[]{:S(2)}, u32[]{:S(2)}) %all-to-all-start.2) | async-done | bytes 147488 | tf_op jit(solution)/shard_map/all_to_all | solution.py:248
  93.3 0.6 reduce_sum.25
Async XLA Ops:
  11.2 17.6 %all-to-all-start = ((bf16[8,6,4,512]{3,2,1,0:T(4,128)(2,1)}), bf16[8,6,4,512]{3,2,1,0:T(4,128)(2,1)S(1)}, u32[]{:S(2)}, u32[]{:S(2)}) async-start(bf16[8,6,4,512]{3,2,1,0:T(4,128)(2,1)} %get-tuple-element.22), calls=%async_computation | async-start | bytes 393216 | tf_op jit(solution)/shard_map/all_to_all | solution.py:212
  41.3 27.8 %all-to-all-start.1 = ((bf16[8,64,768]{2,1,0:T(8,128)(2,1)}), bf16[8,64,768]{2,1,0:T(8,128)(2,1)S(1)}, u32[]{:S(2)}, u32[]{:S(2)}) async-start(bf16[8,64,768]{2,1,0:T(8,128)(2,1)} %get-tuple-element.29), calls=%async_computation.1 | async-start | bytes 1572864 | tf_op jit(solution)/shard_map/all_to_all | solution.py:240
  44.9 4.1 %collective-permute-start = (bf16[4,12,16,384]{3,2,1,0:T(8,128)(2,1)}, bf16[4,12,16,384]{3,2,1,0:T(8,128)(2,1)S(1)}, u32[]{:S(2)}, u32[]{:S(2)}) collective-permute-start(bf16[4,12,16,384]{3,2,1,0:T(8,128)(2,1)} %get-tuple-element.24), channel_id=1, source_target_pairs={{0,16},{16,0},{1,17},{17,1},{2,18},{18,2},{3,19},{19,3},{4,20},{20... | collective-permute-start | bytes 1769480 | tf_op jit(solution)/shard_map/ppermute | solution.py:241
  50.3 11.6 %collective-permute-start.1 = (bf16[12,16,384]{2,1,0:T(8,128)(2,1)S(1)}, bf16[12,16,384]{2,1,0:T(8,128)(2,1)S(1)}, u32[]{:S(2)}, u32[]{:S(2)}) collective-permute-start(bf16[12,16,384]{2,1,0:T(8,128)(2,1)S(1)} %get-tuple-element.26), channel_id=1, source_target_pairs={{0,1},{1,0},{32,33},{33,32},{2,3},{3,2},{34,35},{35,34},{4,5},{5,4... | collective-permute-start | bytes 442376 | tf_op jit(solution)/shard_map/ppermute | solution.py:244
  53.6 11.5 %collective-permute-start.2 = (bf16[12,16,384]{2,1,0:T(8,128)(2,1)S(1)}, bf16[12,16,384]{2,1,0:T(8,128)(2,1)S(1)}, u32[]{:S(2)}, u32[]{:S(2)}) collective-permute-start(bf16[12,16,384]{2,1,0:T(8,128)(2,1)S(1)} %get-tuple-element.27), channel_id=1, source_target_pairs={{0,32},{1,33},{32,0},{33,1},{2,34},{3,35},{34,2},{35,3},{4,36},{5,... | collective-permute-start | bytes 442376 | tf_op jit(solution)/shard_map/ppermute | solution.py:244
  60.0 8.4 %collective-permute-start.3 = (bf16[12,16,384]{2,1,0:T(8,128)(2,1)S(1)}, bf16[12,16,384]{2,1,0:T(8,128)(2,1)S(1)}, u32[]{:S(2)}, u32[]{:S(2)}) collective-permute-start(bf16[12,16,384]{2,1,0:T(8,128)(2,1)S(1)} %get-tuple-element.28), channel_id=1, source_target_pairs={{0,33},{1,32},{32,1},{33,0},{2,35},{3,34},{34,3},{35,2},{4,37},{5,... | collective-permute-start | bytes 442376 | tf_op jit(solution)/shard_map/ppermute | solution.py:244
  69.2 24.2 %all-to-all-start.2 = ((bf16[12,16,384]{2,1,0:T(8,128)(2,1)}), bf16[12,16,384]{2,1,0:T(8,128)(2,1)S(1)}, u32[]{:S(2)}, u32[]{:S(2)}) async-start(bf16[12,16,384]{2,1,0:T(8,128)(2,1)} %add_convert_fusion), calls=%async_computation.2 | async-start | bytes 294912 | tf_op jit(solution)/shard_map/all_to_all | solution.py:248

commit v5 on v4

--- a/solution.py
+++ b/solution.py
@@ -46,16 +46,14 @@
     def _():
         mask_ref[...] = jnp.broadcast_to(clear_ref[...].astype(jnp.float32), (PAIR, cond_rows)).T
 
+    projected = dot(cond_ref[...], jnp.concatenate([wk_ref[...], wv_ref[...]], axis=1))
     for sub in range(STEP):
         lanes = slice(sub * PAIR, (sub + 1) * PAIR)
-        projected = dot(
-            cond_ref[...], jnp.concatenate([wk_ref[:, lanes], wv_ref[:, lanes]], axis=1)
-        )
-        key_raw = projected[:, :PAIR]
+        key_raw = projected[:, lanes]
         keys_ref[:, lanes] = key_raw
         key_normed = key_raw * lax.rsqrt(head_mean(key_raw * key_raw) + NORM_EPSILON)
         key_unit = key_normed.astype(jnp.bfloat16)
-        values = projected[:, PAIR:].astype(jnp.bfloat16)
+        values = projected[:, (STEP + sub) * PAIR : (STEP + sub + 1) * PAIR].astype(jnp.bfloat16)
         q = q_ref[:, lanes].astype(jnp.float32)
         q_unit = (q * lax.rsqrt(head_mean(q * q) + NORM_EPSILON)).astype(jnp.bfloat16)
         first = lax.broadcasted_iota(jnp.int32, key_unit.shape, 1) < DH
@@ -89,6 +87,7 @@
     cond_rows = keys_ref.shape[0]
     step = pl.program_id(0)
     both = []
+    rest = []
     for sub in range(STEP):
         lanes = slice(sub * PAIR, (sub + 1) * PAIR)
         q = q_ref[:, lanes].astype(jnp.float32)
@@ -108,10 +107,7 @@
             probs.append((weights * inverse).astype(jnp.bfloat16))
             dscore = (own_e[at].astype(jnp.float32) - weights * mean) * inverse
             dscores.append(dscore.astype(jnp.bfloat16))
-        gq = [dot(turned[head * DH : (head + 1) * DH], dscores[head]) for head in range(2)]
-        gq = jnp.concatenate(gq, axis=0).T * (DH ** -0.5)
-        gq = q_factor * (gq - q_normed * head_mean(gq * q_normed))
-        gq_ref[:, :, lanes] = gq.astype(gq_ref.dtype).reshape(gq_ref.shape[:2] + (PAIR,))
+        rest.append((lanes, turned, dscores, q_factor, q_normed))
         lane = lax.broadcasted_iota(jnp.int32, (cond_rows, PAIR), 1)
         grad_values = dot(jnp.concatenate(probs, axis=0), g_ref[:, lanes])
         grad_keys = dot(jnp.concatenate(dscores, axis=0), q_unit)
@@ -119,6 +115,11 @@
         gk = jnp.where(lane < DH, grad_keys[:cond_rows], grad_keys[cond_rows:]) * (DH ** -0.5)
         gk_back = key_factor * (gk - key_normed * head_mean(gk * key_normed))
         both += [gk_back.astype(jnp.bfloat16), gv.astype(jnp.bfloat16)]
+    for lanes, turned, dscores, q_factor, q_normed in rest:
+        gq = [dot(turned[head * DH : (head + 1) * DH], dscores[head]) for head in range(2)]
+        gq = jnp.concatenate(gq, axis=0).T * (DH ** -0.5)
+        gq = q_factor * (gq - q_normed * head_mean(gq * q_normed))
+        gq_ref[:, :, lanes] = gq.astype(gq_ref.dtype).reshape(gq_ref.shape[:2] + (PAIR,))
     w_both = []
     for sub in range(STEP):
         lanes = slice(sub * PAIR, (sub + 1) * PAIR)

time: 95.6 us -> 93.9 us (0.982)
  Pallas kernels: 23.1 us -> 21.4 us
    pallas_call x1, Pallas kernels: 10.6 us -> 9.07 us  [body(): pl.pallas_call(scores_kernel, grid=(pairs // STEP,), in_specs=[columns(la...]
where the time goes in v5:
time: 93.9 us; the launch traced here: 92.2 us
  starting transfers between devices  36.5 us (39%)
  waiting for transfers between devices  30.1 us (32%)
  Pallas kernels  21.4 us (23%)
  other arithmetic  3.46 us (4%)
    all_to_all x1, starting transfers between devices, body(): far_parts = lax.all_to_all(near_sum, 'z', 0, 0, tiled=True)  12.3 us
    pallas_call x1, Pallas kernels, body(): pl.pallas_call(grads_kernel, grid=(pairs // STEP,), in_specs=[pl.BlockSpe...  12.3 us
    ppermute x3, starting transfers between devices, body(): lax.ppermute(halves[chip], CHIPS, [(i, i ^ chip) for i in range(chips)])  11.6 us
    all_to_all x1, waiting for transfers between devices, body(): far_parts = lax.all_to_all(near_sum, 'z', 0, 0, tiled=True)  11.1 us
    all_to_all x1, waiting for transfers between devices, body(): sums = lax.all_to_all(sums, 'date', 0, 0, tiled=True)  10.4 us
    pallas_call x1, Pallas kernels, body(): pl.pallas_call(scores_kernel, grid=(pairs // STEP,), in_specs=[columns(la...  9.07 us
    all_to_all x1, starting transfers between devices, body(): sums = lax.all_to_all(sums, 'date', 0, 0, tiled=True)  7.1 us
    ppermute x3, waiting for transfers between devices, body(): lax.ppermute(halves[chip], CHIPS, [(i, i ^ chip) for i in range(chips)])  6.5 us
  transfers between devices with their start and end apart: 7, of which 5 were waited for; matrix products, arithmetic and copies ran while one was open for 3% of the time, Pallas kernels for 0%

profile of v5, /device:TPU:6, one launch (start us, length us, event | category | flops | bytes accessed | tf_op | source)
XLA Modules:
  0.0 92.2 jit_solution(10636488141781621204)
XLA Ops:
  0.6 9.1 %scores.1 = (bf16[8,384,512]{2,1,0:T(8,128)(2,1)}, bf16[8,384,512]{2,1,0:T(8,128)(2,1)}, bf16[4,384,512]{2,1,0:T(8,128)(2,1)S(1)}, bf16[4,384,512]{2,1,0:T(8,128...) custom-call(bf16[512,768]{1,0:T(8,128)(2,1)} %q_ref.3, bf16[512,768]{1,0:T(8,128)(2,1)} %g_ref.3, ...), custom_call_target="tpu_custom_call" | custom-call | tf_op jit(solution)/shard_map/scores/pallas_call | solution.py:188
  9.7 7.1 %all-to-all-start = ((bf16[8,6,4,512]{3,2,1,0:T(4,128)(2,1)}), bf16[8,6,4,512]{3,2,1,0:T(4,128)(2,1)S(1)}, u32[]{:S(2)}, u32[]{:S(2)}) async-start(bf16[8,6,4,512]{3,2,1,0:T(4,128)(2,1)} %get-tuple-element.22), calls=%async_computation | async-start | bytes 393216 | tf_op jit(solution)/shard_map/all_to_all | solution.py:213
  16.8 0.1 pad_add_fusion.place_ref
  16.9 10.4 %all-to-all-done.sums_ref = bf16[8,6,4,512]{3,2,1,0:T(4,128)(2,1)S(1)} async-done(((bf16[8,6,4,512]{3,2,1,0:T(4,128)(2,1)}), bf16[8,6,4,512]{3,2,1,0:T(4,128)(2,1)S(1)}, u32[]{:S(2)}, u32[]{:S(2)}) %all-to-all-start) | async-done | bytes 196640 | tf_op jit(solution)/shard_map/all_to_all | solution.py:213
  27.3 12.3 %grads.1 = (bf16[8,64,768]{2,1,0:T(8,128)(2,1)}, bf16[4,12,16,384]{3,2,1,0:T(8,128)(2,1)}, bf16[4,12,16,384]{3,2,1,0:T(8,128)(2,1)}) custom-call(s32[3]{0:T(128)S(1)} %pad_add_fusion.place_ref, bf16[512,768]{1,0:T(8,128)(2,1)} %q_ref.3, bf16[512,768]{1,0:T(8,128)(2,1)} %g_ref.3, f32[384,768]{1,0:T(8,128)} %get-tuple-element.17.keys_ref, ...), custom_call_target="tpu_custom_call" | custom-call | tf_op jit(solution)/shard_map/grads/pallas_call | solution.py:215
  39.6 3.6 %all-to-all-start.1 = ((bf16[8,64,768]{2,1,0:T(8,128)(2,1)}), bf16[8,64,768]{2,1,0:T(8,128)(2,1)S(1)}, u32[]{:S(2)}, u32[]{:S(2)}) async-start(bf16[8,64,768]{2,1,0:T(8,128)(2,1)} %get-tuple-element.29), calls=%async_computation.1 | async-start | bytes 1572864 | tf_op jit(solution)/shard_map/all_to_all | solution.py:241
  43.2 1.9 %collective-permute-start = (bf16[4,12,16,384]{3,2,1,0:T(8,128)(2,1)}, bf16[4,12,16,384]{3,2,1,0:T(8,128)(2,1)S(1)}, u32[]{:S(2)}, u32[]{:S(2)}) collective-permute-start(bf16[4,12,16,384]{3,2,1,0:T(8,128)(2,1)} %get-tuple-element.24), channel_id=1, source_target_pairs={{0,16},{16,0},{1,17},{17,1},{2,18},{18,2},{3,19},{19,3},{4,20},{20... | collective-permute-start | bytes 1769480 | tf_op jit(solution)/shard_map/ppermute | solution.py:242
  45.1 2.2 %collective-permute-done = bf16[4,12,16,384]{3,2,1,0:T(8,128)(2,1)S(1)} collective-permute-done((bf16[4,12,16,384]{3,2,1,0:T(8,128)(2,1)}, bf16[4,12,16,384]{3,2,1,0:T(8,128)(2,1)S(1)}, u32[]{:S(2)}, u32[]{:S(2)}) %collective-permute-start) | collective-permute-done | bytes 589856 | tf_op jit(solution)/shard_map/ppermute | solution.py:242
  47.3 1.3 %fusion.3 = (bf16[12,16,384]{2,1,0:T(8,128)(2,1)S(1)}, bf16[12,16,384]{2,1,0:T(8,128)(2,1)S(1)}, bf16[12,16,384]{2,1,0:T(8,128)(2,1)S(1)}, bf16[12,16,384]{2,1,0:T(8,128)(2,1)S(1)}) fusion(bf16[4,12,16,384]{3,2,1,0:T(8,128)(2,1)S(1)} %collective-permute-done, bf16[4,12,16,384]{3,2,1,0:T(8,128)(2,1)} %get-tuple-element.23), kind=kLoop, calls=%fused_computation.8 | loop fusion | flops 1179648 | bytes 1769472 | tf_op jit(solution)/shard_map/convert_element_type | solution.py:164
  48.5 3.3 %collective-permute-start.1 = (bf16[12,16,384]{2,1,0:T(8,128)(2,1)S(1)}, bf16[12,16,384]{2,1,0:T(8,128)(2,1)S(1)}, u32[]{:S(2)}, u32[]{:S(2)}) collective-permute-start(bf16[12,16,384]{2,1,0:T(8,128)(2,1)S(1)} %get-tuple-element.26), channel_id=1, source_target_pairs={{0,1},{1,0},{32,33},{33,32},{2,3},{3,2},{34,35},{35,34},{4,5},{5,4... | collective-permute-start | bytes 442376 | tf_op jit(solution)/shard_map/ppermute | solution.py:245
  51.8 6.4 %collective-permute-start.2 = (bf16[12,16,384]{2,1,0:T(8,128)(2,1)S(1)}, bf16[12,16,384]{2,1,0:T(8,128)(2,1)S(1)}, u32[]{:S(2)}, u32[]{:S(2)}) collective-permute-start(bf16[12,16,384]{2,1,0:T(8,128)(2,1)S(1)} %get-tuple-element.27), channel_id=1, source_target_pairs={{0,32},{1,33},{32,0},{33,1},{2,34},{3,35},{34,2},{35,3},{4,36},{5,... | collective-permute-start | bytes 442376 | tf_op jit(solution)/shard_map/ppermute | solution.py:245
  58.2 1.9 %collective-permute-start.3 = (bf16[12,16,384]{2,1,0:T(8,128)(2,1)S(1)}, bf16[12,16,384]{2,1,0:T(8,128)(2,1)S(1)}, u32[]{:S(2)}, u32[]{:S(2)}) collective-permute-start(bf16[12,16,384]{2,1,0:T(8,128)(2,1)S(1)} %get-tuple-element.28), channel_id=1, source_target_pairs={{0,33},{1,32},{32,1},{33,0},{2,35},{3,34},{34,3},{35,2},{4,37},{5,... | collective-permute-start | bytes 442376 | tf_op jit(solution)/shard_map/ppermute | solution.py:245
  60.1 0.0 collective-permute-done.1
  60.2 3.1 %collective-permute-done.2 = bf16[12,16,384]{2,1,0:T(8,128)(2,1)S(1)} collective-permute-done((bf16[12,16,384]{2,1,0:T(8,128)(2,1)S(1)}, bf16[12,16,384]{2,1,0:T(8,128)(2,1)S(1)}, u32[]{:S(2)}, u32[]{:S(2)}) %collective-permute-start.2) | collective-permute-done | bytes 147488 | tf_op jit(solution)/shard_map/ppermute | solution.py:245
  63.3 3.3 %collective-permute-done.3 = bf16[12,16,384]{2,1,0:T(8,128)(2,1)S(1)} collective-permute-done((bf16[12,16,384]{2,1,0:T(8,128)(2,1)S(1)}, bf16[12,16,384]{2,1,0:T(8,128)(2,1)S(1)}, u32[]{:S(2)}, u32[]{:S(2)}) %collective-permute-start.3) | collective-permute-done | bytes 147488 | tf_op jit(solution)/shard_map/ppermute | solution.py:245
  66.7 0.7 add_convert_fusion
  67.4 0.0 all-to-all-done.1
  67.4 12.3 %all-to-all-start.2 = ((bf16[12,16,384]{2,1,0:T(8,128)(2,1)}), bf16[12,16,384]{2,1,0:T(8,128)(2,1)S(1)}, u32[]{:S(2)}, u32[]{:S(2)}) async-start(bf16[12,16,384]{2,1,0:T(8,128)(2,1)} %add_convert_fusion), calls=%async_computation.2 | async-start | bytes 294912 | tf_op jit(solution)/shard_map/all_to_all | solution.py:249
  79.7 0.8 reduce_sum.24
  80.5 11.1 %all-to-all-done.2 = bf16[12,16,384]{2,1,0:T(8,128)(2,1)S(1)} async-done(((bf16[12,16,384]{2,1,0:T(8,128)(2,1)}), bf16[12,16,384]{2,1,0:T(8,128)(2,1)S(1)}, u32[]{:S(2)}, u32[]{:S(2)}) %all-to-all-start.2) | async-done | bytes 147488 | tf_op jit(solution)/shard_map/all_to_all | solution.py:249
  91.6 0.6 reduce_sum.25
Async XLA Ops:
  9.7 17.6 %all-to-all-start = ((bf16[8,6,4,512]{3,2,1,0:T(4,128)(2,1)}), bf16[8,6,4,512]{3,2,1,0:T(4,128)(2,1)S(1)}, u32[]{:S(2)}, u32[]{:S(2)}) async-start(bf16[8,6,4,512]{3,2,1,0:T(4,128)(2,1)} %get-tuple-element.22), calls=%async_computation | async-start | bytes 393216 | tf_op jit(solution)/shard_map/all_to_all | solution.py:213
  39.6 27.8 %all-to-all-start.1 = ((bf16[8,64,768]{2,1,0:T(8,128)(2,1)}), bf16[8,64,768]{2,1,0:T(8,128)(2,1)S(1)}, u32[]{:S(2)}, u32[]{:S(2)}) async-start(bf16[8,64,768]{2,1,0:T(8,128)(2,1)} %get-tuple-element.29), calls=%async_computation.1 | async-start | bytes 1572864 | tf_op jit(solution)/shard_map/all_to_all | solution.py:241
  43.2 4.1 %collective-permute-start = (bf16[4,12,16,384]{3,2,1,0:T(8,128)(2,1)}, bf16[4,12,16,384]{3,2,1,0:T(8,128)(2,1)S(1)}, u32[]{:S(2)}, u32[]{:S(2)}) collective-permute-start(bf16[4,12,16,384]{3,2,1,0:T(8,128)(2,1)} %get-tuple-element.24), channel_id=1, source_target_pairs={{0,16},{16,0},{1,17},{17,1},{2,18},{18,2},{3,19},{19,3},{4,20},{20... | collective-permute-start | bytes 1769480 | tf_op jit(solution)/shard_map/ppermute | solution.py:242
  48.5 11.6 %collective-permute-start.1 = (bf16[12,16,384]{2,1,0:T(8,128)(2,1)S(1)}, bf16[12,16,384]{2,1,0:T(8,128)(2,1)S(1)}, u32[]{:S(2)}, u32[]{:S(2)}) collective-permute-start(bf16[12,16,384]{2,1,0:T(8,128)(2,1)S(1)} %get-tuple-element.26), channel_id=1, source_target_pairs={{0,1},{1,0},{32,33},{33,32},{2,3},{3,2},{34,35},{35,34},{4,5},{5,4... | collective-permute-start | bytes 442376 | tf_op jit(solution)/shard_map/ppermute | solution.py:245
  51.8 11.5 %collective-permute-start.2 = (bf16[12,16,384]{2,1,0:T(8,128)(2,1)S(1)}, bf16[12,16,384]{2,1,0:T(8,128)(2,1)S(1)}, u32[]{:S(2)}, u32[]{:S(2)}) collective-permute-start(bf16[12,16,384]{2,1,0:T(8,128)(2,1)S(1)} %get-tuple-element.27), channel_id=1, source_target_pairs={{0,32},{1,33},{32,0},{33,1},{2,34},{3,35},{34,2},{35,3},{4,36},{5,... | collective-permute-start | bytes 442376 | tf_op jit(solution)/shard_map/ppermute | solution.py:245
  58.2 8.4 %collective-permute-start.3 = (bf16[12,16,384]{2,1,0:T(8,128)(2,1)S(1)}, bf16[12,16,384]{2,1,0:T(8,128)(2,1)S(1)}, u32[]{:S(2)}, u32[]{:S(2)}) collective-permute-start(bf16[12,16,384]{2,1,0:T(8,128)(2,1)S(1)} %get-tuple-element.28), channel_id=1, source_target_pairs={{0,33},{1,32},{32,1},{33,0},{2,35},{3,34},{34,3},{35,2},{4,37},{5,... | collective-permute-start | bytes 442376 | tf_op jit(solution)/shard_map/ppermute | solution.py:245
  67.4 24.2 %all-to-all-start.2 = ((bf16[12,16,384]{2,1,0:T(8,128)(2,1)}), bf16[12,16,384]{2,1,0:T(8,128)(2,1)S(1)}, u32[]{:S(2)}, u32[]{:S(2)}) async-start(bf16[12,16,384]{2,1,0:T(8,128)(2,1)} %add_convert_fusion), calls=%async_computation.2 | async-start | bytes 294912 | tf_op jit(solution)/shard_map/all_to_all | solution.py:249

commit v6 on v5

--- a/solution.py
+++ b/solution.py
@@ -238,9 +238,12 @@
         compiler_params=params,
         name="grads",
     )(place, latent_queries, grad_attention, key_raw, w_key, w_value, weights, carried, near_weights, near_carried, sums)
+    grad_q, stays = lax.optimization_barrier((grad_q, keep[0]))
     share_parts = lax.all_to_all(grad_q, "date", 0, 0, tiled=True)
     other = lax.ppermute(send, "core", [(0, 1), (1, 0)])
-    halves = lax.optimization_barrier([add(keep[chip], other[chip]) for chip in range(chips)])
+    halves = lax.optimization_barrier(
+        [add(stays, other[0])] + [add(keep[chip], other[chip]) for chip in range(1, chips)]
+    )
     near_parts = halves[:1] + [
         lax.ppermute(halves[chip], CHIPS, [(i, i ^ chip) for i in range(chips)])
         for chip in range(1, chips)

time: 93.9 us -> 99.5 us (1.060); the launches traced: 92.2 us -> 99 us
  waiting for transfers between devices: 30.1 us -> 34.2 us
  starting transfers between devices: 36.5 us -> 39.5 us
  other arithmetic: 3.46 us -> 2.33 us
    all_to_all x1, waiting for transfers between devices: 0.01 us -> 4.61 us  [body(): share_parts = lax.all_to_all(grad_q, 'date', 0, 0, tiled=True)]
    all_to_all x1, starting transfers between devices: 12.3 us -> 15.2 us  [body(): far_parts = lax.all_to_all(near_sum, 'z', 0, 0, tiled=True)]
    ppermute x1, waiting for transfers between devices: 2.18 us -> 0.01 us  [body(): other = lax.ppermute(send, 'core', [(0, 1), (1, 0)])]
    all_to_all x1, waiting for transfers between devices: 11.1 us -> 12.3 us  [body(): far_parts = lax.all_to_all(near_sum, 'z', 0, 0, tiled=True)]
    convert_element_type x2 -> x3, other arithmetic: 2.01 us -> 0.88 us  [add(): sum((part.astype(jnp.float32) for part in parts)).astype(jnp.bfloat16)]
where the time goes in v6:
time: 99.5 us; the launch traced here: 99 us
  starting transfers between devices  39.5 us (40%)
  waiting for transfers between devices  34.2 us (34%)
  Pallas kernels  21.4 us (22%)
  other arithmetic  2.33 us (2%)
    all_to_all x1, starting transfers between devices, body(): far_parts = lax.all_to_all(near_sum, 'z', 0, 0, tiled=True)  15.2 us
    all_to_all x1, waiting for transfers between devices, body(): far_parts = lax.all_to_all(near_sum, 'z', 0, 0, tiled=True)  12.3 us
    pallas_call x1, Pallas kernels, body(): pl.pallas_call(grads_kernel, grid=(pairs // STEP,), in_specs=[pl.BlockSpe...  12.3 us
    ppermute x3, starting transfers between devices, body(): lax.ppermute(halves[chip], CHIPS, [(i, i ^ chip) for i in range(chips)])  11.6 us
    all_to_all x1, waiting for transfers between devices, body(): sums = lax.all_to_all(sums, 'date', 0, 0, tiled=True)  10.4 us
    pallas_call x1, Pallas kernels, body(): pl.pallas_call(scores_kernel, grid=(pairs // STEP,), in_specs=[columns(la...  9.03 us
    all_to_all x1, starting transfers between devices, body(): sums = lax.all_to_all(sums, 'date', 0, 0, tiled=True)  7.1 us
    ppermute x3, waiting for transfers between devices, body(): lax.ppermute(halves[chip], CHIPS, [(i, i ^ chip) for i in range(chips)])  6.86 us
  transfers between devices with their start and end apart: 7, of which 5 were waited for; matrix products, arithmetic and copies ran while one was open for 3% of the time, Pallas kernels for 0%

profile of v6, /device:TPU:6, one launch (start us, length us, event | category | flops | bytes accessed | tf_op | source)
XLA Modules:
  0.0 99.0 jit_solution(17667215671968155390)
XLA Ops:
  0.6 9.0 %scores.1 = (bf16[8,384,512]{2,1,0:T(8,128)(2,1)}, bf16[8,384,512]{2,1,0:T(8,128)(2,1)}, bf16[4,384,512]{2,1,0:T(8,128)(2,1)S(1)}, bf16[4,384,512]{2,1,0:T(8,128...) custom-call(bf16[512,768]{1,0:T(8,128)(2,1)} %q_ref.3, bf16[512,768]{1,0:T(8,128)(2,1)} %g_ref.3, ...), custom_call_target="tpu_custom_call" | custom-call | tf_op jit(solution)/shard_map/scores/pallas_call | solution.py:188
  9.7 7.1 %all-to-all-start = ((bf16[8,6,4,512]{3,2,1,0:T(4,128)(2,1)}), bf16[8,6,4,512]{3,2,1,0:T(4,128)(2,1)S(1)}, u32[]{:S(2)}, u32[]{:S(2)}) async-start(bf16[8,6,4,512]{3,2,1,0:T(4,128)(2,1)} %get-tuple-element.24), calls=%async_computation | async-start | bytes 393216 | tf_op jit(solution)/shard_map/all_to_all | solution.py:213
  16.8 0.1 pad_add_fusion.place_ref
  16.8 10.4 %all-to-all-done.sums_ref = bf16[8,6,4,512]{3,2,1,0:T(4,128)(2,1)S(1)} async-done(((bf16[8,6,4,512]{3,2,1,0:T(4,128)(2,1)}), bf16[8,6,4,512]{3,2,1,0:T(4,128)(2,1)S(1)}, u32[]{:S(2)}, u32[]{:S(2)}) %all-to-all-start) | async-done | bytes 196640 | tf_op jit(solution)/shard_map/all_to_all | solution.py:213
  27.2 12.3 %grads.1 = (bf16[8,64,768]{2,1,0:T(8,128)(2,1)}, bf16[4,12,16,384]{3,2,1,0:T(8,128)(2,1)}, bf16[4,12,16,384]{3,2,1,0:T(8,128)(2,1)}) custom-call(s32[3]{0:T(128)S(1)} %pad_add_fusion.place_ref, bf16[512,768]{1,0:T(8,128)(2,1)} %q_ref.3, bf16[512,768]{1,0:T(8,128)(2,1)} %g_ref.3, f32[384,768]{1,0:T(8,128)} %get-tuple-element.19.keys_ref, ...), custom_call_target="tpu_custom_call" | custom-call | tf_op jit(solution)/shard_map/grads/pallas_call | solution.py:215
  39.6 0.0 copy-start
  39.6 2.1 %collective-permute-start = (bf16[4,12,16,384]{3,2,1,0:T(8,128)(2,1)}, bf16[4,12,16,384]{3,2,1,0:T(8,128)(2,1)S(1)}, u32[]{:S(2)}, u32[]{:S(2)}) collective-permute-start(bf16[4,12,16,384]{3,2,1,0:T(8,128)(2,1)} %get-tuple-element.28), channel_id=1, source_target_pairs={{0,16},{16,0},{1,17},{17,1},{2,18},{18,2},{3,19},{19,3},{4,20},{20... | collective-permute-start | bytes 1769480 | tf_op jit(solution)/shard_map/ppermute | solution.py:243
  41.6 0.9 slice_bitcast_fusion.1
  42.6 3.6 %all-to-all-start.1 = ((bf16[8,64,768]{2,1,0:T(8,128)(2,1)}), bf16[8,64,768]{2,1,0:T(8,128)(2,1)S(1)}, u32[]{:S(2)}, u32[]{:S(2)}) async-start(bf16[8,64,768]{2,1,0:T(8,128)(2,1)} %get-tuple-element.33), calls=%async_computation.1 | async-start | bytes 1572864 | tf_op jit(solution)/shard_map/all_to_all | solution.py:242
  46.1 0.0 collective-permute-done
  46.2 0.0 copy-done
  46.2 0.1 fusion.3
  46.3 3.3 %collective-permute-start.1 = (bf16[12,16,384]{2,1,0:T(8,128)(2,1)S(1)}, bf16[12,16,384]{2,1,0:T(8,128)(2,1)S(1)}, u32[]{:S(2)}, u32[]{:S(2)}) collective-permute-start(bf16[12,16,384]{2,1,0:T(8,128)(2,1)S(1)} %get-tuple-element.30), channel_id=1, source_target_pairs={{0,1},{1,0},{32,33},{33,32},{2,3},{3,2},{34,35},{35,34},{4,5},{5,4... | collective-permute-start | bytes 442376 | tf_op jit(solution)/shard_map/ppermute | solution.py:248
  49.6 6.4 %collective-permute-start.2 = (bf16[12,16,384]{2,1,0:T(8,128)(2,1)S(1)}, bf16[12,16,384]{2,1,0:T(8,128)(2,1)S(1)}, u32[]{:S(2)}, u32[]{:S(2)}) collective-permute-start(bf16[12,16,384]{2,1,0:T(8,128)(2,1)S(1)} %get-tuple-element.31), channel_id=1, source_target_pairs={{0,32},{1,33},{32,0},{33,1},{2,34},{3,35},{34,2},{35,3},{4,36},{5,... | collective-permute-start | bytes 442376 | tf_op jit(solution)/shard_map/ppermute | solution.py:248
  56.0 1.9 %collective-permute-start.3 = (bf16[12,16,384]{2,1,0:T(8,128)(2,1)S(1)}, bf16[12,16,384]{2,1,0:T(8,128)(2,1)S(1)}, u32[]{:S(2)}, u32[]{:S(2)}) collective-permute-start(bf16[12,16,384]{2,1,0:T(8,128)(2,1)S(1)} %get-tuple-element.32), channel_id=1, source_target_pairs={{0,33},{1,32},{32,1},{33,0},{2,35},{3,34},{34,3},{35,2},{4,37},{5,... | collective-permute-start | bytes 442376 | tf_op jit(solution)/shard_map/ppermute | solution.py:248
  57.9 0.0 collective-permute-done.1
  57.9 3.5 %collective-permute-done.2 = bf16[12,16,384]{2,1,0:T(8,128)(2,1)S(1)} collective-permute-done((bf16[12,16,384]{2,1,0:T(8,128)(2,1)S(1)}, bf16[12,16,384]{2,1,0:T(8,128)(2,1)S(1)}, u32[]{:S(2)}, u32[]{:S(2)}) %collective-permute-start.2) | collective-permute-done | bytes 147488 | tf_op jit(solution)/shard_map/ppermute | solution.py:248
  61.4 3.3 %collective-permute-done.3 = bf16[12,16,384]{2,1,0:T(8,128)(2,1)S(1)} collective-permute-done((bf16[12,16,384]{2,1,0:T(8,128)(2,1)S(1)}, bf16[12,16,384]{2,1,0:T(8,128)(2,1)S(1)}, u32[]{:S(2)}, u32[]{:S(2)}) %collective-permute-start.3) | collective-permute-done | bytes 147488 | tf_op jit(solution)/shard_map/ppermute | solution.py:248
  64.8 0.7 add_convert_fusion
  65.5 4.6 %all-to-all-done.1 = bf16[8,64,768]{2,1,0:T(8,128)(2,1)S(1)} async-done(((bf16[8,64,768]{2,1,0:T(8,128)(2,1)}), bf16[8,64,768]{2,1,0:T(8,128)(2,1)S(1)}, u32[]{:S(2)}, u32[]{:S(2)}) %all-to-all-start.1) | async-done | bytes 786464 | tf_op jit(solution)/shard_map/all_to_all | solution.py:242
  70.1 15.2 %all-to-all-start.2 = ((bf16[12,16,384]{2,1,0:T(8,128)(2,1)}), bf16[12,16,384]{2,1,0:T(8,128)(2,1)S(1)}, u32[]{:S(2)}, u32[]{:S(2)}) async-start(bf16[12,16,384]{2,1,0:T(8,128)(2,1)} %add_convert_fusion), calls=%async_computation.2 | async-start | bytes 294912 | tf_op jit(solution)/shard_map/all_to_all | solution.py:252
  85.3 0.8 reduce_sum.24
  86.1 12.3 %all-to-all-done.2 = bf16[12,16,384]{2,1,0:T(8,128)(2,1)S(1)} async-done(((bf16[12,16,384]{2,1,0:T(8,128)(2,1)}), bf16[12,16,384]{2,1,0:T(8,128)(2,1)S(1)}, u32[]{:S(2)}, u32[]{:S(2)}) %all-to-all-start.2) | async-done | bytes 147488 | tf_op jit(solution)/shard_map/all_to_all | solution.py:252
  98.4 0.6 reduce_sum.25
  (1 shorter events, 0.0 us)
Async XLA Ops:
  9.7 17.6 %all-to-all-start = ((bf16[8,6,4,512]{3,2,1,0:T(4,128)(2,1)}), bf16[8,6,4,512]{3,2,1,0:T(4,128)(2,1)S(1)}, u32[]{:S(2)}, u32[]{:S(2)}) async-start(bf16[8,6,4,512]{3,2,1,0:T(4,128)(2,1)} %get-tuple-element.24), calls=%async_computation | async-start | bytes 393216 | tf_op jit(solution)/shard_map/all_to_all | solution.py:213
  39.6 6.6 %copy-start = (bf16[4,12,16,384]{3,2,1,0:T(8,128)(2,1)S(1)}, bf16[4,12,16,384]{3,2,1,0:T(8,128)(2,1)}, u32[]{:S(2)}) copy-start(bf16[4,12,16,384]{3,2,1,0:T(8,128)(2,1)} %get-tuple-element.26) | copy-start | bytes 1769476
  39.6 6.6 %collective-permute-start = (bf16[4,12,16,384]{3,2,1,0:T(8,128)(2,1)}, bf16[4,12,16,384]{3,2,1,0:T(8,128)(2,1)S(1)}, u32[]{:S(2)}, u32[]{:S(2)}) collective-permute-start(bf16[4,12,16,384]{3,2,1,0:T(8,128)(2,1)} %get-tuple-element.28), channel_id=1, source_target_pairs={{0,16},{16,0},{1,17},{17,1},{2,18},{18,2},{3,19},{19,3},{4,20},{20... | collective-permute-start | bytes 1769480 | tf_op jit(solution)/shard_map/ppermute | solution.py:243
  42.6 27.6 %all-to-all-start.1 = ((bf16[8,64,768]{2,1,0:T(8,128)(2,1)}), bf16[8,64,768]{2,1,0:T(8,128)(2,1)S(1)}, u32[]{:S(2)}, u32[]{:S(2)}) async-start(bf16[8,64,768]{2,1,0:T(8,128)(2,1)} %get-tuple-element.33), calls=%async_computation.1 | async-start | bytes 1572864 | tf_op jit(solution)/shard_map/all_to_all | solution.py:242
  46.3 11.6 %collective-permute-start.1 = (bf16[12,16,384]{2,1,0:T(8,128)(2,1)S(1)}, bf16[12,16,384]{2,1,0:T(8,128)(2,1)S(1)}, u32[]{:S(2)}, u32[]{:S(2)}) collective-permute-start(bf16[12,16,384]{2,1,0:T(8,128)(2,1)S(1)} %get-tuple-element.30), channel_id=1, source_target_pairs={{0,1},{1,0},{32,33},{33,32},{2,3},{3,2},{34,35},{35,34},{4,5},{5,4... | collective-permute-start | bytes 442376 | tf_op jit(solution)/shard_map/ppermute | solution.py:248
  49.6 11.8 %collective-permute-start.2 = (bf16[12,16,384]{2,1,0:T(8,128)(2,1)S(1)}, bf16[12,16,384]{2,1,0:T(8,128)(2,1)S(1)}, u32[]{:S(2)}, u32[]{:S(2)}) collective-permute-start(bf16[12,16,384]{2,1,0:T(8,128)(2,1)S(1)} %get-tuple-element.31), channel_id=1, source_target_pairs={{0,32},{1,33},{32,0},{33,1},{2,34},{3,35},{34,2},{35,3},{4,36},{5,... | collective-permute-start | bytes 442376 | tf_op jit(solution)/shard_map/ppermute | solution.py:248
  56.0 8.8 %collective-permute-start.3 = (bf16[12,16,384]{2,1,0:T(8,128)(2,1)S(1)}, bf16[12,16,384]{2,1,0:T(8,128)(2,1)S(1)}, u32[]{:S(2)}, u32[]{:S(2)}) collective-permute-start(bf16[12,16,384]{2,1,0:T(8,128)(2,1)S(1)} %get-tuple-element.32), channel_id=1, source_target_pairs={{0,33},{1,32},{32,1},{33,0},{2,35},{3,34},{34,3},{35,2},{4,37},{5,... | collective-permute-start | bytes 442376 | tf_op jit(solution)/shard_map/ppermute | solution.py:248
  70.1 28.2 %all-to-all-start.2 = ((bf16[12,16,384]{2,1,0:T(8,128)(2,1)}), bf16[12,16,384]{2,1,0:T(8,128)(2,1)S(1)}, u32[]{:S(2)}, u32[]{:S(2)}) async-start(bf16[12,16,384]{2,1,0:T(8,128)(2,1)} %add_convert_fusion), calls=%async_computation.2 | async-start | bytes 294912 | tf_op jit(solution)/shard_map/all_to_all | solution.py:252

commit v7 on v5

--- a/solution.py
+++ b/solution.py
@@ -97,7 +97,7 @@
         key_raw = keys_ref[:, lanes]
         key_factor = lax.rsqrt(head_mean(key_raw * key_raw) + NORM_EPSILON)
         key_normed = key_raw * key_factor
-        turned = key_normed.T.astype(jnp.bfloat16)
+        turned = key_normed.astype(jnp.bfloat16).T
         probs = []
         dscores = []
         for head in range(2):

time: 93.9 us -> 93.8 us (level)
  no operation moved by 1% of the time
where the time goes in v7:
time: 93.8 us; the launch traced here: 92.1 us
  starting transfers between devices  36.5 us (39%)
  waiting for transfers between devices  30.1 us (32%)
  Pallas kernels  21.3 us (23%)
  other arithmetic  3.46 us (4%)
    all_to_all x1, starting transfers between devices, body(): far_parts = lax.all_to_all(near_sum, 'z', 0, 0, tiled=True)  12.3 us
    pallas_call x1, Pallas kernels, body(): pl.pallas_call(grads_kernel, grid=(pairs // STEP,), in_specs=[pl.BlockSpe...  12.2 us
    ppermute x3, starting transfers between devices, body(): lax.ppermute(halves[chip], CHIPS, [(i, i ^ chip) for i in range(chips)])  11.6 us
    all_to_all x1, waiting for transfers between devices, body(): far_parts = lax.all_to_all(near_sum, 'z', 0, 0, tiled=True)  11.1 us
    all_to_all x1, waiting for transfers between devices, body(): sums = lax.all_to_all(sums, 'date', 0, 0, tiled=True)  10.4 us
    pallas_call x1, Pallas kernels, body(): pl.pallas_call(scores_kernel, grid=(pairs // STEP,), in_specs=[columns(la...  9.07 us
    all_to_all x1, starting transfers between devices, body(): sums = lax.all_to_all(sums, 'date', 0, 0, tiled=True)  7.1 us
    ppermute x3, waiting for transfers between devices, body(): lax.ppermute(halves[chip], CHIPS, [(i, i ^ chip) for i in range(chips)])  6.5 us
  transfers between devices with their start and end apart: 7, of which 5 were waited for; matrix products, arithmetic and copies ran while one was open for 3% of the time, Pallas kernels for 0%

profile of v7, /device:TPU:6, one launch (start us, length us, event | category | flops | bytes accessed | tf_op | source)
XLA Modules:
  0.0 92.1 jit_solution(5733742630779135669)
XLA Ops:
  0.6 9.1 %scores.1 = (bf16[8,384,512]{2,1,0:T(8,128)(2,1)}, bf16[8,384,512]{2,1,0:T(8,128)(2,1)}, bf16[4,384,512]{2,1,0:T(8,128)(2,1)S(1)}, bf16[4,384,512]{2,1,0:T(8,128...) custom-call(bf16[512,768]{1,0:T(8,128)(2,1)} %q_ref.3, bf16[512,768]{1,0:T(8,128)(2,1)} %g_ref.3, ...), custom_call_target="tpu_custom_call" | custom-call | tf_op jit(solution)/shard_map/scores/pallas_call | solution.py:188
  9.7 7.1 %all-to-all-start = ((bf16[8,6,4,512]{3,2,1,0:T(4,128)(2,1)}), bf16[8,6,4,512]{3,2,1,0:T(4,128)(2,1)S(1)}, u32[]{:S(2)}, u32[]{:S(2)}) async-start(bf16[8,6,4,512]{3,2,1,0:T(4,128)(2,1)} %get-tuple-element.22), calls=%async_computation | async-start | bytes 393216 | tf_op jit(solution)/shard_map/all_to_all | solution.py:213
  16.8 0.1 pad_add_fusion.place_ref
  16.9 10.4 %all-to-all-done.sums_ref = bf16[8,6,4,512]{3,2,1,0:T(4,128)(2,1)S(1)} async-done(((bf16[8,6,4,512]{3,2,1,0:T(4,128)(2,1)}), bf16[8,6,4,512]{3,2,1,0:T(4,128)(2,1)S(1)}, u32[]{:S(2)}, u32[]{:S(2)}) %all-to-all-start) | async-done | bytes 196640 | tf_op jit(solution)/shard_map/all_to_all | solution.py:213
  27.3 12.2 %grads.1 = (bf16[8,64,768]{2,1,0:T(8,128)(2,1)}, bf16[4,12,16,384]{3,2,1,0:T(8,128)(2,1)}, bf16[4,12,16,384]{3,2,1,0:T(8,128)(2,1)}) custom-call(s32[3]{0:T(128)S(1)} %pad_add_fusion.place_ref, bf16[512,768]{1,0:T(8,128)(2,1)} %q_ref.3, bf16[512,768]{1,0:T(8,128)(2,1)} %g_ref.3, f32[384,768]{1,0:T(8,128)} %get-tuple-element.17.keys_ref, ...), custom_call_target="tpu_custom_call" | custom-call | tf_op jit(solution)/shard_map/grads/pallas_call | solution.py:215
  39.5 3.6 %all-to-all-start.1 = ((bf16[8,64,768]{2,1,0:T(8,128)(2,1)}), bf16[8,64,768]{2,1,0:T(8,128)(2,1)S(1)}, u32[]{:S(2)}, u32[]{:S(2)}) async-start(bf16[8,64,768]{2,1,0:T(8,128)(2,1)} %get-tuple-element.29), calls=%async_computation.1 | async-start | bytes 1572864 | tf_op jit(solution)/shard_map/all_to_all | solution.py:241
  43.0 1.9 %collective-permute-start = (bf16[4,12,16,384]{3,2,1,0:T(8,128)(2,1)}, bf16[4,12,16,384]{3,2,1,0:T(8,128)(2,1)S(1)}, u32[]{:S(2)}, u32[]{:S(2)}) collective-permute-start(bf16[4,12,16,384]{3,2,1,0:T(8,128)(2,1)} %get-tuple-element.24), channel_id=1, source_target_pairs={{0,16},{16,0},{1,17},{17,1},{2,18},{18,2},{3,19},{19,3},{4,20},{20... | collective-permute-start | bytes 1769480 | tf_op jit(solution)/shard_map/ppermute | solution.py:242
  45.0 2.2 %collective-permute-done = bf16[4,12,16,384]{3,2,1,0:T(8,128)(2,1)S(1)} collective-permute-done((bf16[4,12,16,384]{3,2,1,0:T(8,128)(2,1)}, bf16[4,12,16,384]{3,2,1,0:T(8,128)(2,1)S(1)}, u32[]{:S(2)}, u32[]{:S(2)}) %collective-permute-start) | collective-permute-done | bytes 589856 | tf_op jit(solution)/shard_map/ppermute | solution.py:242
  47.2 1.3 %fusion.3 = (bf16[12,16,384]{2,1,0:T(8,128)(2,1)S(1)}, bf16[12,16,384]{2,1,0:T(8,128)(2,1)S(1)}, bf16[12,16,384]{2,1,0:T(8,128)(2,1)S(1)}, bf16[12,16,384]{2,1,0:T(8,128)(2,1)S(1)}) fusion(bf16[4,12,16,384]{3,2,1,0:T(8,128)(2,1)S(1)} %collective-permute-done, bf16[4,12,16,384]{3,2,1,0:T(8,128)(2,1)} %get-tuple-element.23), kind=kLoop, calls=%fused_computation.8 | loop fusion | flops 1179648 | bytes 1769472 | tf_op jit(solution)/shard_map/convert_element_type | solution.py:164
  48.4 3.3 %collective-permute-start.1 = (bf16[12,16,384]{2,1,0:T(8,128)(2,1)S(1)}, bf16[12,16,384]{2,1,0:T(8,128)(2,1)S(1)}, u32[]{:S(2)}, u32[]{:S(2)}) collective-permute-start(bf16[12,16,384]{2,1,0:T(8,128)(2,1)S(1)} %get-tuple-element.26), channel_id=1, source_target_pairs={{0,1},{1,0},{32,33},{33,32},{2,3},{3,2},{34,35},{35,34},{4,5},{5,4... | collective-permute-start | bytes 442376 | tf_op jit(solution)/shard_map/ppermute | solution.py:245
  51.8 6.4 %collective-permute-start.2 = (bf16[12,16,384]{2,1,0:T(8,128)(2,1)S(1)}, bf16[12,16,384]{2,1,0:T(8,128)(2,1)S(1)}, u32[]{:S(2)}, u32[]{:S(2)}) collective-permute-start(bf16[12,16,384]{2,1,0:T(8,128)(2,1)S(1)} %get-tuple-element.27), channel_id=1, source_target_pairs={{0,32},{1,33},{32,0},{33,1},{2,34},{3,35},{34,2},{35,3},{4,36},{5,... | collective-permute-start | bytes 442376 | tf_op jit(solution)/shard_map/ppermute | solution.py:245
  58.1 1.9 %collective-permute-start.3 = (bf16[12,16,384]{2,1,0:T(8,128)(2,1)S(1)}, bf16[12,16,384]{2,1,0:T(8,128)(2,1)S(1)}, u32[]{:S(2)}, u32[]{:S(2)}) collective-permute-start(bf16[12,16,384]{2,1,0:T(8,128)(2,1)S(1)} %get-tuple-element.28), channel_id=1, source_target_pairs={{0,33},{1,32},{32,1},{33,0},{2,35},{3,34},{34,3},{35,2},{4,37},{5,... | collective-permute-start | bytes 442376 | tf_op jit(solution)/shard_map/ppermute | solution.py:245
  60.0 0.0 collective-permute-done.1
  60.1 3.1 %collective-permute-done.2 = bf16[12,16,384]{2,1,0:T(8,128)(2,1)S(1)} collective-permute-done((bf16[12,16,384]{2,1,0:T(8,128)(2,1)S(1)}, bf16[12,16,384]{2,1,0:T(8,128)(2,1)S(1)}, u32[]{:S(2)}, u32[]{:S(2)}) %collective-permute-start.2) | collective-permute-done | bytes 147488 | tf_op jit(solution)/shard_map/ppermute | solution.py:245
  63.2 3.3 %collective-permute-done.3 = bf16[12,16,384]{2,1,0:T(8,128)(2,1)S(1)} collective-permute-done((bf16[12,16,384]{2,1,0:T(8,128)(2,1)S(1)}, bf16[12,16,384]{2,1,0:T(8,128)(2,1)S(1)}, u32[]{:S(2)}, u32[]{:S(2)}) %collective-permute-start.3) | collective-permute-done | bytes 147488 | tf_op jit(solution)/shard_map/ppermute | solution.py:245
  66.5 0.7 add_convert_fusion
  67.3 0.0 all-to-all-done.1
  67.3 12.3 %all-to-all-start.2 = ((bf16[12,16,384]{2,1,0:T(8,128)(2,1)}), bf16[12,16,384]{2,1,0:T(8,128)(2,1)S(1)}, u32[]{:S(2)}, u32[]{:S(2)}) async-start(bf16[12,16,384]{2,1,0:T(8,128)(2,1)} %add_convert_fusion), calls=%async_computation.2 | async-start | bytes 294912 | tf_op jit(solution)/shard_map/all_to_all | solution.py:249
  79.6 0.8 reduce_sum.24
  80.4 11.1 %all-to-all-done.2 = bf16[12,16,384]{2,1,0:T(8,128)(2,1)S(1)} async-done(((bf16[12,16,384]{2,1,0:T(8,128)(2,1)}), bf16[12,16,384]{2,1,0:T(8,128)(2,1)S(1)}, u32[]{:S(2)}, u32[]{:S(2)}) %all-to-all-start.2) | async-done | bytes 147488 | tf_op jit(solution)/shard_map/all_to_all | solution.py:249
  91.5 0.6 reduce_sum.25
Async XLA Ops:
  9.7 17.6 %all-to-all-start = ((bf16[8,6,4,512]{3,2,1,0:T(4,128)(2,1)}), bf16[8,6,4,512]{3,2,1,0:T(4,128)(2,1)S(1)}, u32[]{:S(2)}, u32[]{:S(2)}) async-start(bf16[8,6,4,512]{3,2,1,0:T(4,128)(2,1)} %get-tuple-element.22), calls=%async_computation | async-start | bytes 393216 | tf_op jit(solution)/shard_map/all_to_all | solution.py:213
  39.5 27.8 %all-to-all-start.1 = ((bf16[8,64,768]{2,1,0:T(8,128)(2,1)}), bf16[8,64,768]{2,1,0:T(8,128)(2,1)S(1)}, u32[]{:S(2)}, u32[]{:S(2)}) async-start(bf16[8,64,768]{2,1,0:T(8,128)(2,1)} %get-tuple-element.29), calls=%async_computation.1 | async-start | bytes 1572864 | tf_op jit(solution)/shard_map/all_to_all | solution.py:241
  43.0 4.1 %collective-permute-start = (bf16[4,12,16,384]{3,2,1,0:T(8,128)(2,1)}, bf16[4,12,16,384]{3,2,1,0:T(8,128)(2,1)S(1)}, u32[]{:S(2)}, u32[]{:S(2)}) collective-permute-start(bf16[4,12,16,384]{3,2,1,0:T(8,128)(2,1)} %get-tuple-element.24), channel_id=1, source_target_pairs={{0,16},{16,0},{1,17},{17,1},{2,18},{18,2},{3,19},{19,3},{4,20},{20... | collective-permute-start | bytes 1769480 | tf_op jit(solution)/shard_map/ppermute | solution.py:242
  48.4 11.6 %collective-permute-start.1 = (bf16[12,16,384]{2,1,0:T(8,128)(2,1)S(1)}, bf16[12,16,384]{2,1,0:T(8,128)(2,1)S(1)}, u32[]{:S(2)}, u32[]{:S(2)}) collective-permute-start(bf16[12,16,384]{2,1,0:T(8,128)(2,1)S(1)} %get-tuple-element.26), channel_id=1, source_target_pairs={{0,1},{1,0},{32,33},{33,32},{2,3},{3,2},{34,35},{35,34},{4,5},{5,4... | collective-permute-start | bytes 442376 | tf_op jit(solution)/shard_map/ppermute | solution.py:245
  51.8 11.5 %collective-permute-start.2 = (bf16[12,16,384]{2,1,0:T(8,128)(2,1)S(1)}, bf16[12,16,384]{2,1,0:T(8,128)(2,1)S(1)}, u32[]{:S(2)}, u32[]{:S(2)}) collective-permute-start(bf16[12,16,384]{2,1,0:T(8,128)(2,1)S(1)} %get-tuple-element.27), channel_id=1, source_target_pairs={{0,32},{1,33},{32,0},{33,1},{2,34},{3,35},{34,2},{35,3},{4,36},{5,... | collective-permute-start | bytes 442376 | tf_op jit(solution)/shard_map/ppermute | solution.py:245
  58.1 8.4 %collective-permute-start.3 = (bf16[12,16,384]{2,1,0:T(8,128)(2,1)S(1)}, bf16[12,16,384]{2,1,0:T(8,128)(2,1)S(1)}, u32[]{:S(2)}, u32[]{:S(2)}) collective-permute-start(bf16[12,16,384]{2,1,0:T(8,128)(2,1)S(1)} %get-tuple-element.28), channel_id=1, source_target_pairs={{0,33},{1,32},{32,1},{33,0},{2,35},{3,34},{34,3},{35,2},{4,37},{5,... | collective-permute-start | bytes 442376 | tf_op jit(solution)/shard_map/ppermute | solution.py:245
  67.3 24.2 %all-to-all-start.2 = ((bf16[12,16,384]{2,1,0:T(8,128)(2,1)}), bf16[12,16,384]{2,1,0:T(8,128)(2,1)S(1)}, u32[]{:S(2)}, u32[]{:S(2)}) async-start(bf16[12,16,384]{2,1,0:T(8,128)(2,1)} %add_convert_fusion), calls=%async_computation.2 | async-start | bytes 294912 | tf_op jit(solution)/shard_map/all_to_all | solution.py:249
